TPU v7x, 32 devices: a whole 2x2x4 slice. The times are simulated.
32 devices in a mesh: row: 8 (over y, x, core), col: 4 (over z).
Axes of the slice: x: 2, y: 2, z: 4, core: 2. Of those that a mesh axis runs over, the one named last changes fastest.
Arguments:
- tiles: bfloat16 [8192, 128, 128], P(('row', 'col'))
- tile_src: int32 [8192], P(('row', 'col')), may hold values from 0 to 15
- tile_slot: int32 [8192], P(('row', 'col')), may hold values from 0 to 127
- slot_block: int32 [4096], P(('row', 'col')), may hold values from 0 to 15
- out_degree: int32 [65536], P(('row', 'col')), may hold values from 512 to 2047
- good_seeds: int32 [128, 4096], P(None, ('row', 'col')), may hold values from 0 to 65535, as said below
- spam_cores: int32 [128, 2048], P(None, ('row', 'col')), may hold values from 0 to 65535, as said below
Outputs:
- trust: float32 [65536, 128], P(('row', 'col'))
- distrust: float32 [65536, 128], P(('row', 'col'))
Inputs may be any that keep to these rules, and one draw needn't show every extreme that they name: `tile_slot`: slot s of a device belongs to the peer with index s // 4 along row+col. `slot_block`: entry p * 128 + s is the local index, among the 16 blocks held by peer s // 4, of the target block of slot s of device p. `good_seeds`: entries j * 128 to (j + 1) * 128 - 1 of each column's list are hosts of device j, from j * 2048 to (j + 1) * 2048 - 1. `spam_cores`: entries j * 64 to (j + 1) * 64 - 1 of each column's list are hosts of device j, from j * 2048 to (j + 1) * 2048 - 1.
All inputs are finite; a program needn't handle non-finite values.
Results may differ from a plain program's by a relative error of at most 0.0003.
Values may be sent and summed in bfloat16 or wider, within the bound.
A program may use at most 128 MiB of HBM per device.

v0:
```python
import jax
import jax.numpy as jnp
from jax import lax
from jax.sharding import PartitionSpec as P

TRUST_ITERS = 2
ANTI_ITERS = 2


def teleport(seeds, host_count, factor):
    column_index = jnp.broadcast_to(
        jnp.arange(seeds.shape[0], dtype=jnp.int32)[:, None], seeds.shape
    )
    counts = (
        jnp.zeros((host_count, seeds.shape[0]), jnp.float32)
        .at[seeds % host_count, column_index]
        .add(jnp.float32(1.0))
    )
    return counts * jnp.float32(factor)


def first_push(outgoing, col_terms, slot_ids):
    return (
        lax.all_to_all(outgoing, ("row", "col"), split_axis=0, concat_axis=0, tiled=True),
        lax.all_to_all(col_terms, ("row", "col"), split_axis=0, concat_axis=0, tiled=True),
        lax.all_to_all(slot_ids, ("row", "col"), split_axis=0, concat_axis=0, tiled=True),
    )


def later_push(outgoing):
    return lax.all_to_all(outgoing, ("row", "col"), split_axis=0, concat_axis=0, tiled=True)


def pull_shares(outgoing):
    return lax.all_to_all(outgoing, ("row", "col"), split_axis=0, concat_axis=0, tiled=True)


def body(tiles, tile_src, tile_slot, slot_block, out_degree, good_seeds, spam_cores):
    tile_size = tiles.shape[1]
    host_count = out_degree.shape[0]
    block_count = host_count // tile_size
    column_count = good_seeds.shape[0]
    slot_count = slot_block.shape[0]
    good_start = teleport(good_seeds, host_count, host_count / good_seeds.shape[1])
    spam_start = teleport(spam_cores, host_count, host_count / spam_cores.shape[1])
    col_terms = jax.ops.segment_sum(
        jnp.sum(tiles, axis=1, dtype=jnp.float32), tile_slot, num_segments=slot_count
    )
    slot_ids = slot_block.astype(jnp.float32)
    degree = out_degree.astype(jnp.float32)[:, None]
    trust = good_start
    block_ids = jnp.zeros((slot_count,), jnp.int32)
    in_weight = jnp.ones((host_count,), jnp.float32)
    for iteration in range(TRUST_ITERS):
        scaled = (trust / degree).astype(jnp.bfloat16)
        sources = scaled.reshape(block_count, tile_size, column_count)[tile_src]
        products = jnp.einsum("kij,kis->kjs", tiles, sources, preferred_element_type=jnp.float32)
        outgoing = jax.ops.segment_sum(products, tile_slot, num_segments=slot_count)
        if iteration == 0:
            arrived, arrived_cols, arrived_ids = first_push(outgoing, col_terms, slot_ids)
            block_ids = arrived_ids.astype(jnp.int32)
            in_weight = 1.0 + jax.ops.segment_sum(
                arrived_cols, block_ids, num_segments=block_count
            ).reshape(host_count)
        else:
            arrived = later_push(outgoing)
        inflow = jax.ops.segment_sum(arrived, block_ids, num_segments=block_count).reshape(
            host_count, column_count
        )
        trust = 0.85 * inflow + 0.15 * good_start
    shield = 1.0 / (1.0 + trust)
    distrust = spam_start
    for iteration in range(ANTI_ITERS):
        share = (shield * distrust / in_weight[:, None]).astype(jnp.bfloat16)
        requested = share.reshape(block_count, tile_size, column_count)[block_ids]
        fetched = pull_shares(requested)
        targets = fetched[tile_slot]
        products = jnp.einsum("kij,kjs->kis", tiles, targets, preferred_element_type=jnp.float32)
        gathered_back = jax.ops.segment_sum(products, tile_src, num_segments=block_count).reshape(
            host_count, column_count
        )
        distrust = 0.85 * gathered_back + 0.15 * spam_start
    return (trust, distrust)


def solution(mesh):
    in_specs = (
        P(("row", "col"), None, None),
        P(("row", "col")),
        P(("row", "col")),
        P(("row", "col")),
        P(("row", "col")),
        P(None, ("row", "col")),
        P(None, ("row", "col")),
    )
    out_specs = (P(("row", "col"), None), P(("row", "col"), None))
    return jax.shard_map(body, mesh=mesh, in_specs=in_specs, out_specs=out_specs, check_vma=False)
```

profile of v0, /device:TPU:1, one launch (start us, length us, event | category | flops | bytes accessed | tf_op | source)
XLA Modules:
  0.0 1069.4 jit_solution(13790211607943945537)
XLA Ops:
  2.0 7.1 all-to-all-start
  12.9 86.1 %scatter_custom_fusion.8 = f32[262144]{0:T(1024)S(1)} fusion(s32[16384]{0:T(1024)S(1)} %select_bitcast_fusion, f32[16384]{0:T(1024)S(1)} %broadcast.152, f32[]{:T(128)} %constant.17.clone.1), kind=kCustom, calls=%fused_computation.38 | custom fusion | flops 16384 | bytes 1048580
  99.3 8.6 gather_fusion
  107.9 14.4 %convolution_bitcast_fusion.3 = f32[256,128,128]{1,2,0:T(8,128)} fusion(bf16[256,128,128]{2,1,0:T(8,128)(2,1)} %gather_fusion, bf16[256,128,128]{2,1,0:T(8,128)(2,1)} %param.7), kind=kOutput, calls=%fused_computation.20 | convolution fusion | flops 1073741824 | bytes 33554432 | tf_op jit(solution)/shard_map/kij,kis->kjs/dot_general | solution.py:57
  122.3 17.5 %copy.23 = f32[256,128,128]{2,1,0:T(8,128)} copy(f32[256,128,128]{1,2,0:T(8,128)} %convolution_bitcast_fusion.3) | data formatting | bytes 33554432 | tf_op jit(solution)/shard_map/kij,kis->kjs/dot_general | solution.py:57
  139.8 4.3 broadcast.115.clone
  144.1 51.8 %scatter_fusion = f32[128,128,128]{2,1,0:T(8,128)} fusion(f32[128,128,128]{2,1,0:T(8,128)} %broadcast.115.clone, s32[256]{0:T(256)S(1)} %copy-done.2, f32[256,128,128]{2,1,0:T(8,128)} %copy.23), kind=kCustom, calls=%fused_computation.6 | custom fusion | flops 4194304 | bytes 50332672 | tf_op jit(solution)/shard_map/scatter-add | solution.py:58
  195.9 6.4 all-to-all-start.1
  202.2 6.2 convert_reduce_fusion
  210.6 171.5 %all-to-all-done.1 = f32[128,128,128]{2,1,0:T(8,128)} async-done(((f32[128,128,128]{2,1,0:T(8,128)}), f32[128,128,128]{2,1,0:T(8,128)}, u32[]{:S(2)}, u32[]{:S(2)}) %all-to-all-start.1) | async-done | bytes 8388640 | tf_op jit(solution)/shard_map/all_to_all | solution.py:24
  382.1 9.8 all-to-all-start.3
  392.0 17.0 %scatter_fusion.1 = f32[16,128,128]{2,1,0:T(8,128)S(1)} fusion(f32[16,128,128]{2,1,0:T(8,128)S(1)} %broadcast.114.clone.1, s32[128]{0:T(128)S(1)} %reshape.183, f32[128,128,128]{2,1,0:T(8,128)} %all-to-all-done.1), kind=kCustom, calls=%fused_computation.7 | custom fusion | flops 2097152 | bytes 25166336 | tf_op jit(solution)/shard_map/scatter-add | solution.py:67
  409.5 8.6 gather_fusion.1
  418.1 14.4 %convolution_bitcast_fusion.2 = f32[256,128,128]{1,2,0:T(8,128)} fusion(bf16[256,128,128]{2,1,0:T(8,128)(2,1)} %gather_fusion.1, bf16[256,128,128]{2,1,0:T(8,128)(2,1)} %param.7), kind=kOutput, calls=%fused_computation.19 | convolution fusion | flops 1073741824 | bytes 33554432 | tf_op jit(solution)/shard_map/kij,kis->kjs/dot_general | solution.py:57
  432.4 17.5 %copy.25 = f32[256,128,128]{2,1,0:T(8,128)} copy(f32[256,128,128]{1,2,0:T(8,128)} %convolution_bitcast_fusion.2) | data formatting | bytes 33554432 | tf_op jit(solution)/shard_map/kij,kis->kjs/dot_general | solution.py:57
  449.9 4.3 broadcast.115
  454.2 51.8 %scatter_fusion.2 = f32[128,128,128]{2,1,0:T(8,128)} fusion(f32[128,128,128]{2,1,0:T(8,128)} %broadcast.115, s32[256]{0:T(256)S(1)} %copy-done.2, f32[256,128,128]{2,1,0:T(8,128)} %copy.25), kind=kCustom, calls=%fused_computation.8 | custom fusion | flops 4194304 | bytes 50332672 | tf_op jit(solution)/shard_map/scatter-add | solution.py:58
  506.0 6.0 all-to-all-start.2
  512.4 43.5 %scatter_custom_fusion.9 = f32[262144]{0:T(1024)S(1)} fusion(s32[8192]{0:T(1024)S(1)} %reshape.227, f32[8192]{0:T(1024)S(1)} %broadcast.154, f32[]{:T(128)} %constant.17.clone.1), kind=kCustom, calls=%fused_computation.36 | custom fusion | flops 8192 | bytes 1048580
  557.3 134.8 %all-to-all-done.2 = f32[128,128,128]{2,1,0:T(8,128)} async-done(((f32[128,128,128]{2,1,0:T(8,128)}), f32[128,128,128]{2,1,0:T(8,128)}, u32[]{:S(2)}, u32[]{:S(2)}) %all-to-all-start.2) | async-done | bytes 8388640 | tf_op jit(solution)/shard_map/all_to_all | solution.py:31
  692.2 17.0 %scatter_fusion.3 = f32[16,128,128]{2,1,0:T(8,128)S(1)} fusion(f32[16,128,128]{2,1,0:T(8,128)S(1)} %broadcast.114.clone, s32[128]{0:T(128)S(1)} %reshape.183, f32[128,128,128]{2,1,0:T(8,128)} %all-to-all-done.2), kind=kCustom, calls=%fused_computation.9 | custom fusion | flops 2097152 | bytes 25166336 | tf_op jit(solution)/shard_map/scatter-add | solution.py:67
  713.7 9.8 all-to-all-start.4
  723.5 92.0 %all-to-all-done.4 = bf16[128,128,128]{2,1,0:T(8,128)(2,1)} async-done(((bf16[128,128,128]{2,1,0:T(8,128)(2,1)}), bf16[128,128,128]{2,1,0:T(8,128)(2,1)}, u32[]{:S(2)}, u32[]{:S(2)}) %all-to-all-start.4) | async-done | bytes 4194336 | tf_op jit(solution)/shard_map/all_to_all | solution.py:35
  815.5 10.8 %gather_fusion.3 = bf16[256,128,128]{2,1,0:T(8,128)(2,1)} fusion(bf16[128,128,128]{2,1,0:T(8,128)(2,1)} %all-to-all-done.4, s32[1024]{0:T(1024)S(1)} %pad_clamp_fusion), kind=kCustom, calls=%fused_computation.3 | custom fusion | bytes 16778240 | tf_op jit(solution)/shard_map/gather | solution.py:77
  826.3 12.8 %convolution_bitcast_fusion.1 = f32[256,128,128]{1,2,0:T(8,128)} fusion(bf16[256,128,128]{2,1,0:T(8,128)(2,1)} %gather_fusion.3, bf16[256,128,128]{2,1,0:T(8,128)(2,1)} %param.7), kind=kOutput, calls=%fused_computation.18 | convolution fusion | flops 1073741824 | bytes 33554432 | tf_op jit(solution)/shard_map/kij,kjs->kis/dot_general | solution.py:78
  839.2 17.5 %copy.28 = f32[256,128,128]{2,1,0:T(8,128)} copy(f32[256,128,128]{1,2,0:T(8,128)} %convolution_bitcast_fusion.1) | data formatting | bytes 33554432 | tf_op jit(solution)/shard_map/kij,kjs->kis/dot_general | solution.py:78
  856.8 33.2 %scatter_fusion.4 = f32[16,128,128]{2,1,0:T(8,128)S(1)} fusion(f32[16,128,128]{2,1,0:T(8,128)S(1)} %broadcast.114.clone.2, s32[256]{0:T(256)S(1)} %copy-done.3, f32[256,128,128]{2,1,0:T(8,128)} %copy.28), kind=kCustom, calls=%fused_computation.12 | custom fusion | flops 4194304 | bytes 50332672 | tf_op jit(solution)/shard_map/scatter-add | solution.py:79
  893.5 99.9 %all_to_all.41 = bf16[128,128,128]{2,1,0:T(8,128)(2,1)} all-to-all(bf16[128,128,128]{2,1,0:T(8,128)(2,1)} %gather_fusion.4), channel_id=1, replica_groups=mesh['row'=8,'col'=4] {'row','col'}, dimensions={0} | all-to-all | bytes 8388608 | tf_op jit(solution)/shard_map/all_to_all | solution.py:35
  993.4 10.8 %gather_fusion.5 = bf16[256,128,128]{2,1,0:T(8,128)(2,1)} fusion(bf16[128,128,128]{2,1,0:T(8,128)(2,1)} %all_to_all.41, s32[1024]{0:T(1024)S(1)} %pad_clamp_fusion), kind=kCustom, calls=%fused_computation.5 | custom fusion | bytes 16778240 | tf_op jit(solution)/shard_map/gather | solution.py:77
  1004.2 12.8 %convolution_bitcast_fusion = f32[256,128,128]{1,2,0:T(8,128)} fusion(bf16[256,128,128]{2,1,0:T(8,128)(2,1)} %gather_fusion.5, bf16[256,128,128]{2,1,0:T(8,128)(2,1)} %param.7), kind=kOutput, calls=%fused_computation.17 | convolution fusion | flops 1073741824 | bytes 33554432 | tf_op jit(solution)/shard_map/kij,kjs->kis/dot_general | solution.py:78
  1017.0 17.5 %copy.30 = f32[256,128,128]{2,1,0:T(8,128)} copy(f32[256,128,128]{1,2,0:T(8,128)} %convolution_bitcast_fusion) | data formatting | bytes 33554432 | tf_op jit(solution)/shard_map/kij,kjs->kis/dot_general | solution.py:78
  1034.6 33.2 %scatter_fusion.5 = f32[16,128,128]{2,1,0:T(8,128)S(1)} fusion(f32[16,128,128]{2,1,0:T(8,128)S(1)} %broadcast.114, s32[256]{0:T(256)S(1)} %copy-done.3, f32[256,128,128]{2,1,0:T(8,128)} %copy.30), kind=kCustom, calls=%fused_computation.13 | custom fusion | flops 4194304 | bytes 50332672 | tf_op jit(solution)/shard_map/scatter-add | solution.py:79
  (58 shorter events, 19.4 us)
Async XLA Ops:
  2.0 193.9 %all-to-all-start = ((f32[32,4,1]{1,2,0:T(1,128)}), f32[32,4,1]{1,2,0:T(1,128)S(1)}, u32[]{:S(2)}, u32[]{:S(2)}) async-start(f32[32,4,1]{1,2,0:T(1,128)} %bitcast), calls=%async_computation | async-start | bytes 32768 | tf_op jit(solution)/shard_map/all_to_all | solution.py:26
  139.8 4.3 copy-start.2
  195.9 186.2 %all-to-all-start.1 = ((f32[128,128,128]{2,1,0:T(8,128)}), f32[128,128,128]{2,1,0:T(8,128)}, u32[]{:S(2)}, u32[]{:S(2)}) async-start(f32[128,128,128]{2,1,0:T(8,128)} %scatter_fusion), calls=%async_computation.1 | async-start | bytes 16777216 | tf_op jit(solution)/shard_map/all_to_all | solution.py:24
  382.1 123.9 %all-to-all-start.3 = ((f32[32,4,128]{2,1,0:T(4,128)}), f32[32,4,128]{2,1,0:T(4,128)S(1)}, u32[]{:S(2)}, u32[]{:S(2)}) async-start(f32[32,4,128]{2,1,0:T(4,128)} %bitcast.13), calls=%async_computation.3 | async-start | bytes 131072 | tf_op jit(solution)/shard_map/all_to_all | solution.py:25
  506.0 6.1 copy-start.1
  506.0 6.1 copy-start.4
  506.0 6.2 copy-start.5
  506.0 186.1 %all-to-all-start.2 = ((f32[128,128,128]{2,1,0:T(8,128)}), f32[128,128,128]{2,1,0:T(8,128)}, u32[]{:S(2)}, u32[]{:S(2)}) async-start(f32[128,128,128]{2,1,0:T(8,128)} %scatter_fusion.2), calls=%async_computation.2 | async-start | bytes 16777216 | tf_op jit(solution)/shard_map/all_to_all | solution.py:31
  713.7 101.9 %all-to-all-start.4 = ((bf16[128,128,128]{2,1,0:T(8,128)(2,1)}), bf16[128,128,128]{2,1,0:T(8,128)(2,1)}, u32[]{:S(2)}, u32[]{:S(2)}) async-start(bf16[128,128,128]{2,1,0:T(8,128)(2,1)} %gather_fusion.2), calls=%async_computation.4 | async-start | bytes 8388608 | tf_op jit(solution)/shard_map/all_to_all | solution.py:35
  839.2 17.6 %copy-start.3 = (s32[256]{0:T(256)S(1)}, s32[256]{0:T(256)}, u32[]{:S(2)}) copy-start(s32[256]{0:T(256)} %param.8) | copy-start | bytes 3076
  856.7 33.3 %copy-start = (f32[2048,128]{1,0:T(8,128)S(1)}, f32[2048,128]{1,0:T(8,128)}, u32[]{:S(2)}) copy-start(f32[2048,128]{1,0:T(8,128)} %get-tuple-element.3) | copy-start | bytes 3145732
where the time goes:
time: 1080 us; the launch traced here: 1070 us
  waiting for transfers between devices  398 us (37%)
  other arithmetic  352 us (33%)
  local copies, waits for them, and re-layouts  125 us (12%)
  blocking collectives  99.9 us (9%)
  matrix products  54.4 us (5%)
  starting transfers between devices  39.1 us (4%)
    all_to_all x1, waiting for transfers between devices, first_push(): lax.all_to_all(outgoing, ('row', 'col'), split_axis=0, concat_axis=0, til...  171 us
    all_to_all x1, waiting for transfers between devices, later_push(): lax.all_to_all(outgoing, ('row', 'col'), split_axis=0, concat_axis=0, til...  135 us
    unnamed x8, other arithmetic  131 us
    scatter-add x2, other arithmetic, body(): outgoing = jax.ops.segment_sum(products, tile_slot, num_segments=slot_count)  104 us
    all_to_all x1, blocking collectives, pull_shares(): lax.all_to_all(outgoing, ('row', 'col'), split_axis=0, concat_axis=0, til...  99.9 us
    all_to_all x1, waiting for transfers between devices, pull_shares(): lax.all_to_all(outgoing, ('row', 'col'), split_axis=0, concat_axis=0, til...  92 us
    scatter-add x2, other arithmetic, body(): jax.ops.segment_sum(products, tile_src, num_segments=block_count)  66.4 us
    dot_general x2, local copies, waits for them, and re-layouts, body(): jnp.einsum('kij,kjs->kis', tiles, targets, preferred_element_type=jnp.flo...  34.9 us
  transfers between devices with their start and end apart: 5, of which 3 were waited for; matrix products, arithmetic and copies ran while one was open for 33% of the time, Pallas kernels for 0%

commit v1 on v0

v1 whole, which is shorter than its diff:
```python
import functools

import jax
import jax.numpy as jnp
from jax import lax
from jax.experimental import pallas as pl
from jax.experimental.pallas import tpu as pltpu
from jax.sharding import PartitionSpec as P

AXES = ("row", "col")
VM = pl.BlockSpec(memory_space=pltpu.VMEM)
SM = pl.BlockSpec(memory_space=pltpu.SMEM)
F32 = jnp.float32
BF16 = jnp.bfloat16
WORD = 15


def seed_kernel(columns, good_seeds_ref, spam_cores_ref, good_ref, spam_ref):
    blocks, seeds, size = good_ref.shape
    hosts = blocks * size
    base = (lax.axis_index("row") * columns + lax.axis_index("col")) * hosts
    for source, target in ((good_seeds_ref, good_ref), (spam_cores_ref, spam_ref)):
        count = source.shape[1]
        factor = F32(hosts / count)
        block_iota = lax.broadcasted_iota(jnp.int32, (blocks, count), 0) * size
        lane_iota = lax.broadcasted_iota(jnp.int32, (size, count), 0)

        def one(s, _):
            local = source[pl.ds(s, 1), :] - base
            shifted = local - block_iota
            inside = jnp.where((shifted >= 0) & (shifted < size), F32(1), F32(0)).astype(BF16)
            start = jnp.max(jnp.where(local >= block_iota, block_iota, 0), axis=0, keepdims=True)
            lane = jnp.where(lane_iota == local - start, F32(1), F32(0)).astype(BF16)
            counts = lax.dot_general(
                inside, lane, (((1,), (1,)), ((), ())), preferred_element_type=F32
            )
            for b in range(blocks):
                target[b, pl.ds(s, 1), :] = counts[b : b + 1, :] * factor
            return 0

        lax.fori_loop(0, seeds, one, 0, unroll=4)


def exponent_of(peak):
    return jnp.floor(jnp.log2(jnp.maximum(peak, F32(2.0**-100)))) + F32(1)


def to_words(value):
    return jnp.clip(jnp.floor(value + F32(0.5)), F32(-32767), F32(32767))


def pack(first, cap, acc, out_ref):
    peers = out_ref.shape[0]
    size = acc.shape[2]
    tail = out_ref.shape[1] - cap * size

    def one(p, _):
        exps, cols = [], []
        for c in range(cap):
            n = p * cap + c
            value = acc[n, :size, :]
            e = exponent_of(jnp.max(jnp.abs(value), axis=0, keepdims=True))
            out_ref[p, c * size : (c + 1) * size, :] = to_words(value * jnp.exp2(WORD - e)).astype(
                jnp.int32
            ).astype(jnp.int16)
            exps.append(e)
            if first:
                col = acc[n, size : size + 8, :][:1, :]
                f = exponent_of(jnp.abs(col))
                scaled = col * jnp.exp2(WORD - f)
                high = to_words(scaled)
                cols += [f, high, to_words((scaled - high) * F32(2.0**WORD))]
        rows = exps + cols
        if tail > len(rows):
            rows.append(jnp.zeros((tail - len(rows), size), F32))
        out_ref[p, cap * size :, :] = jnp.concatenate(rows, axis=0).astype(jnp.int32).astype(jnp.int16)
        return 0

    lax.fori_loop(0, peers, one, 0)


def unpack(cap, ids_ref, arrived_ref, inflow, weight):
    peers = arrived_ref.shape[0]
    size = inflow.shape[2]
    inflow[...] = jnp.zeros_like(inflow)
    if weight is not None:
        weight[...] = jnp.ones_like(weight)

    def one(p, _):
        rows = arrived_ref[p, cap * size :, :].astype(jnp.int32).astype(F32)
        for c in range(cap):
            b = ids_ref[p * cap + c]
            value = arrived_ref[p, c * size : (c + 1) * size, :].astype(jnp.int32).astype(F32)
            inflow[b] += value * jnp.exp2(rows[c : c + 1, :] - WORD)
            if weight is not None:
                at = cap + 3 * c
                f, high, low = (rows[at + i : at + i + 1, :] for i in range(3))
                weight[b] += (high + low * F32(2.0**-WORD)) * jnp.exp2(f - WORD)
        return 0

    lax.fori_loop(0, peers, one, 0)


def push_kernel(first, cap, *refs):
    if first:
        src_ref, slot_ref, good_ref, degree_ref, tiles_ref, out_ref, acc, scaled = refs
    else:
        (src_ref, slot_ref, ids_ref, arrived_ref, good_ref, degree_ref, tiles_ref,
         out_ref, weight_ref, acc, scaled, inflow) = refs
    step = pl.program_id(0)
    blocks, seeds, size = good_ref.shape
    per_step = tiles_ref.shape[0]

    @pl.when(step == 0)
    def _():
        acc[...] = jnp.zeros_like(acc)
        if not first:
            unpack(cap, ids_ref, arrived_ref, inflow, weight_ref)

        def one(b, _):
            degree = degree_ref[b].astype(F32)
            trust = good_ref[b]
            if not first:
                trust = F32(0.85) * inflow[b] + F32(0.15) * trust
            scaled[b, :seeds, :] = (trust / degree).astype(BF16)
            if first:
                scaled[b, seeds:, :] = jnp.ones((scaled.shape[1] - seeds, size), BF16)
            return 0

        lax.fori_loop(0, blocks, one, 0)

    def one(k, _):
        n = step * per_step + k
        acc[slot_ref[n]] += jnp.dot(scaled[src_ref[n]], tiles_ref[k], preferred_element_type=F32)
        return 0

    lax.fori_loop(0, per_step, one, 0, unroll=4)

    @pl.when(step == pl.num_programs(0) - 1)
    def _():
        pack(first, cap, acc, out_ref)


def shares(ids_ref, shield_ref, weight_ref, start_of, share, asked_ref):
    def one(b, _):
        share[b] = (shield_ref[b] * start_of(b) / weight_ref[b]).astype(BF16)
        return 0

    lax.fori_loop(0, share.shape[0], one, 0)

    def ask(n, _):
        asked_ref[n] = share[ids_ref[n]]
        return 0

    lax.fori_loop(0, asked_ref.shape[0], ask, 0)


def trust_kernel(cap, ids_ref, arrived_ref, good_ref, spam_ref, weight_ref,
                 trust_ref, shield_ref, asked_ref, inflow, share):
    unpack(cap, ids_ref, arrived_ref, inflow, None)
    size = inflow.shape[2]

    def one(b, _):
        trust = F32(0.85) * inflow[b] + F32(0.15) * good_ref[b]
        trust_ref[pl.ds(pl.multiple_of(b * size, size), size), :] = jnp.transpose(trust)
        shield_ref[b] = F32(1) / (F32(1) + trust)
        return 0

    lax.fori_loop(0, inflow.shape[0], one, 0)
    shares(ids_ref, shield_ref, weight_ref, lambda b: spam_ref[b], share, asked_ref)


def pull_kernel(last, *refs):
    if last:
        src_ref, slot_ref, fetched_ref, spam_ref, tiles_ref, out_ref, acc = refs
    else:
        (src_ref, slot_ref, ids_ref, fetched_ref, spam_ref, shield_ref, weight_ref, tiles_ref,
         out_ref, acc, share) = refs
    step = pl.program_id(0)
    per_step = tiles_ref.shape[0]
    size = acc.shape[2]

    @pl.when(step == 0)
    def _():
        acc[...] = jnp.zeros_like(acc)

    def one(k, _):
        n = step * per_step + k
        acc[src_ref[n]] += lax.dot_general(
            fetched_ref[slot_ref[n]], tiles_ref[k], (((1,), (1,)), ((), ())),
            preferred_element_type=F32,
        )
        return 0

    lax.fori_loop(0, per_step, one, 0, unroll=4)

    @pl.when(step == pl.num_programs(0) - 1)
    def _():
        def distrust(b):
            return F32(0.85) * acc[b] + F32(0.15) * spam_ref[b]

        if last:
            def one(b, _):
                out_ref[pl.ds(pl.multiple_of(b * size, size), size), :] = jnp.transpose(distrust(b))
                return 0

            lax.fori_loop(0, acc.shape[0], one, 0)
        else:
            shares(ids_ref, shield_ref, weight_ref, distrust, share, out_ref)


def body(columns, tiles, tile_src, tile_slot, slot_block, out_degree, good_seeds, spam_cores):
    tile_count, size, _ = tiles.shape
    hosts = out_degree.shape[0]
    blocks = hosts // size
    seeds = good_seeds.shape[0]
    slots = slot_block.shape[0]
    peers = lax.axis_size(AXES)
    cap = slots // peers
    tail = -(-4 * cap // 16) * 16
    steps = 8
    shape = jax.ShapeDtypeStruct
    vector = (blocks, seeds, size)
    degree = out_degree.reshape(blocks, 1, size)

    def exchange(x):
        return lax.all_to_all(x, AXES, split_axis=0, concat_axis=0, tiled=True)

    ids = exchange(slot_block.reshape(peers, cap)).reshape(slots)
    good, spam = pl.pallas_call(
        functools.partial(seed_kernel, columns),
        out_shape=(shape(vector, F32), shape(vector, F32)),
        in_specs=[VM, VM],
        out_specs=(VM, VM),
    )(good_seeds, spam_cores)

    tile_spec = pl.BlockSpec((tile_count // steps, size, size), lambda i: (i, 0, 0))
    words = shape((peers, cap * size + tail, size), jnp.int16)
    outgoing = pl.pallas_call(
        functools.partial(push_kernel, True, cap),
        grid=(steps,),
        out_shape=words,
        in_specs=[SM, SM, VM, VM, tile_spec],
        out_specs=VM,
        scratch_shapes=[
            pltpu.VMEM((slots, seeds + 16, size), F32),
            pltpu.VMEM((blocks, seeds + 16, size), BF16),
        ],
    )(tile_src, tile_slot, good, degree, tiles)
    arrived = exchange(outgoing)
    outgoing, weight = pl.pallas_call(
        functools.partial(push_kernel, False, cap),
        grid=(steps,),
        out_shape=(words, shape((blocks, 1, size), F32)),
        in_specs=[SM, SM, SM, VM, VM, VM, tile_spec],
        out_specs=(VM, VM),
        scratch_shapes=[
            pltpu.VMEM((slots, seeds, size), F32),
            pltpu.VMEM(vector, BF16),
            pltpu.VMEM(vector, F32),
        ],
    )(tile_src, tile_slot, ids, arrived, good, degree, tiles)
    arrived = exchange(outgoing)
    asked_shape = shape((slots, seeds, size), BF16)
    trust, shield, asked = pl.pallas_call(
        functools.partial(trust_kernel, cap),
        out_shape=(shape((hosts, seeds), F32), shape(vector, F32), asked_shape),
        in_specs=[SM, VM, VM, VM, VM],
        out_specs=(VM, VM, VM),
        scratch_shapes=[pltpu.VMEM(vector, F32), pltpu.VMEM(vector, BF16)],
    )(ids, arrived, good, spam, weight)
    fetched = exchange(asked)
    asked = pl.pallas_call(
        functools.partial(pull_kernel, False),
        grid=(steps,),
        out_shape=asked_shape,
        in_specs=[SM, SM, SM, VM, VM, VM, VM, tile_spec],
        out_specs=VM,
        scratch_shapes=[pltpu.VMEM(vector, F32), pltpu.VMEM(vector, BF16)],
    )(tile_src, tile_slot, ids, fetched, spam, shield, weight, tiles)
    fetched = exchange(asked)
    distrust = pl.pallas_call(
        functools.partial(pull_kernel, True),
        grid=(steps,),
        out_shape=shape((hosts, seeds), F32),
        in_specs=[SM, SM, VM, VM, tile_spec],
        out_specs=VM,
        scratch_shapes=[pltpu.VMEM(vector, F32)],
    )(tile_src, tile_slot, fetched, spam, tiles)
    return trust, distrust


def solution(mesh):
    in_specs = (
        P(AXES, None, None),
        P(AXES),
        P(AXES),
        P(AXES),
        P(AXES),
        P(None, AXES),
        P(None, AXES),
    )
    out_specs = (P(AXES, None), P(AXES, None))
    return jax.shard_map(
        functools.partial(body, mesh.shape["col"]),
        mesh=mesh, in_specs=in_specs, out_specs=out_specs, check_vma=False,
    )
```

time: 1080 us -> 521 us (0.48)
  other arithmetic: 352 us -> 0.69 us
  waiting for transfers between devices: 398 us -> 92.8 us
  blocking collectives: 99.9 us -> 298 us
  local copies, waits for them, and re-layouts: 125 us -> 4.05 us
  Pallas kernels: 0 us -> 111 us
  matrix products: 54.4 us -> 0 us
  starting transfers between devices: 39.1 us -> 12.9 us
    all_to_all x5 -> x2, waiting for transfers between devices: 398 us -> 92.8 us  [exchange(): return lax.all_to_all(x, AXES, split_axis=0, concat_axis=0, tiled=True)]
    scatter-add x8 -> x0, other arithmetic: 207 us -> none  [the longest x2 104 us: body(): outgoing = jax.ops.segment_sum(products, tile_slot, num_segments=slot_count)]
    all_to_all x1 -> x3, blocking collectives: 99.9 us -> 298 us  [exchange(): return lax.all_to_all(x, AXES, split_axis=0, concat_axis=0, tiled=True)]
    unnamed x8 -> x0, other arithmetic: 131 us -> none
    pallas_call x0 -> x6, Pallas kernels: none -> 111 us  [the longest x1 23.2 us: body(): pl.pallas_call(functools.partial(push_kernel, True, cap), grid=(steps,),...]
    dot_general x4 -> x0, local copies, waits for them, and re-layouts: 69.9 us -> none  [the longest x2 34.9 us: body(): jnp.einsum('kij,kjs->kis', tiles, targets, preferred_element_type=jnp.flo...]
    dot_general x4 -> x0, matrix products: 54.4 us -> none  [the longest x2 28.7 us: body(): jnp.einsum('kij,kis->kjs', tiles, sources, preferred_element_type=jnp.flo...]
    gather x6 -> x0, local copies, waits for them, and re-layouts: 44.9 us -> none  [the longest x2 21.6 us: body(): targets = fetched[tile_slot]]
  transfers between devices with their start and end apart: 5 -> 2, of which waited for: 3 -> 1; matrix products, arithmetic and copies ran while one was open for 33% -> 1% of each run, Pallas kernels for 0% -> 7%
where the time goes in v1:
time: 521 us; the launch traced here: 520 us
  blocking collectives  298 us (57%)
  Pallas kernels  111 us (21%)
  waiting for transfers between devices  92.8 us (18%)
  starting transfers between devices  12.9 us (2%)
    all_to_all x3, blocking collectives, exchange(): return lax.all_to_all(x, AXES, split_axis=0, concat_axis=0, tiled=True)  298 us
    all_to_all x2, waiting for transfers between devices, exchange(): return lax.all_to_all(x, AXES, split_axis=0, concat_axis=0, tiled=True)  92.8 us
    pallas_call x1, Pallas kernels, body(): pl.pallas_call(functools.partial(push_kernel, True, cap), grid=(steps,),...  23.2 us
    pallas_call x1, Pallas kernels, body(): pl.pallas_call(functools.partial(push_kernel, False, cap), grid=(steps,),...  22.7 us
    pallas_call x1, Pallas kernels, body(): pl.pallas_call(functools.partial(pull_kernel, False), grid=(steps,), out_...  20.6 us
    pallas_call x1, Pallas kernels, body(): pl.pallas_call(functools.partial(pull_kernel, True), grid=(steps,), out_s...  19.6 us
    pallas_call x1, Pallas kernels, body(): pl.pallas_call(functools.partial(seed_kernel, columns), out_shape=(shape(...  15.3 us
    all_to_all x2, starting transfers between devices, exchange(): return lax.all_to_all(x, AXES, split_axis=0, concat_axis=0, tiled=True)  12.9 us
  transfers between devices with their start and end apart: 2, of which 1 were waited for; matrix products, arithmetic and copies ran while one was open for 1% of the time, Pallas kernels for 7%

profile of v1, /device:TPU:1, one launch (start us, length us, event | category | flops | bytes accessed | tf_op | source)
XLA Modules:
  0.0 520.4 jit_solution(6217555233025260559)
XLA Ops:
  0.6 1.4 all_to_all.18
  2.0 7.1 %all-to-all-start = ((s32[32,1,4]{2,1,0:T(1,128)}), s32[32,1,4]{2,1,0:T(1,128)S(1)}, u32[]{:S(2)}, u32[]{:S(2)}) async-start(s32[32,1,4]{2,1,0:T(1,128)} %bitcast), calls=%async_computation | async-start | bytes 32768 | tf_op jit(solution)/shard_map/all_to_all | solution.py:227
  9.1 1.5 copy.12.spam_cores_ref
  10.6 15.3 %shard_map.86 = (f32[16,128,128]{2,1,0:T(8,128)}, f32[16,128,128]{2,1,0:T(8,128)}) custom-call(s32[128,128]{1,0:T(8,128)} %good_seeds_ref.1, s32[128,64]{1,0:T(8,128)} %copy.12.spam_cores_ref), custom_call_target="tpu_custom_call" | custom-call | tf_op jit(solution)/shard_map/pallas_call | solution.py:230
  25.9 23.2 %shard_map.87 = s16[32,528,128]{2,1,0:T(8,128)(2,1)} custom-call(s32[256]{0:T(256)} %refs_0_.7, s32[256]{0:T(256)} %refs_1_.7, f32[16,128,128]{2,1,0:T(8,128)} %get-tuple-element.9.refs_2_.refs_4_.good_ref, s32[16,1,128]{2,1,0:T(1,128)} %bitcast.2, bf16[256,128,128]{2,1,0:T(8,128)(2,1)} %refs_4_.3), custom_call_target="tpu_custom_call" | custom-call | tf_op jit(solution)/shard_map/pallas_call | solution.py:239
  49.1 0.0 all-to-all-done
  49.1 5.9 %all-to-all-start.1 = ((s16[32,528,128]{2,1,0:T(8,128)(2,1)}), s16[32,528,128]{2,1,0:T(8,128)(2,1)}, u32[]{:S(2)}, u32[]{:S(2)}) async-start(s16[32,528,128]{2,1,0:T(8,128)(2,1)} %shard_map.87), calls=%async_computation.1 | async-start | bytes 8650752 | tf_op jit(solution)/shard_map/all_to_all | solution.py:227
  54.9 0.5 broadcast.3
  55.5 0.7 reduce.3
  56.1 0.7 reshape.15.refs_2_.ids_ref
  56.8 92.8 %all-to-all-done.1.refs_3_ = s16[32,528,128]{2,1,0:T(8,128)(2,1)} async-done(((s16[32,528,128]{2,1,0:T(8,128)(2,1)}), s16[32,528,128]{2,1,0:T(8,128)(2,1)}, u32[]{:S(2)}, u32[]{:S(2)}) %all-to-all-start.1) | async-done | bytes 4325408 | tf_op jit(solution)/shard_map/all_to_all | solution.py:227
  149.7 22.7 %shard_map.88 = (s16[32,528,128]{2,1,0:T(8,128)(2,1)}, f32[16,1,128]{2,1,0:T(1,128)}) custom-call(s32[256]{0:T(256)} %refs_0_.7, s32[256]{0:T(256)} %refs_1_.7, s32[128]{0:T(128)} %reshape.15.refs_2_.ids_ref, s16[32,528,128]{2,1,0:T(8,128)(2,1)} %all-to-all-done.1.refs_3_, f32[16,128,128]{2,1,0:T(8,128)} %get-tuple-element.9.refs_2_.refs_4_.good_ref, ...), custom_call_target="tpu_custom_call" | custom-call | tf_op jit(solution)/shard_map/pallas_call | solution.py:251
  172.4 103.6 %all_to_all.29.arrived_ref = s16[32,528,128]{2,1,0:T(8,128)(2,1)} all-to-all(s16[32,528,128]{2,1,0:T(8,128)(2,1)} %get-tuple-element.10), channel_id=1, replica_groups=mesh['row'=8,'col'=4] {'row','col'}, dimensions={0} | all-to-all | bytes 8650752 | tf_op jit(solution)/shard_map/all_to_all | solution.py:227
  276.0 9.8 %shard_map.89 = (f32[2048,128]{1,0:T(8,128)}, f32[16,128,128]{2,1,0:T(8,128)}, bf16[128,128,128]{2,1,0:T(8,128)(2,1)}) custom-call(s32[128]{0:T(128)} %reshape.15.refs_2_.ids_ref, s16[32,528,128]{2,1,0:T(8,128)(2,1)} %all_to_all.29.arrived_ref, f32[16,128,128]{2,1,0:T(8,128)} %get-tuple-element.9.refs_2_.refs_4_.good_ref, ...), custom_call_target="tpu_custom_call" | custom-call | tf_op jit(solution)/shard_map/pallas_call | solution.py:265
  285.9 97.3 %all_to_all.30.refs_3_ = bf16[128,128,128]{2,1,0:T(8,128)(2,1)} all-to-all(bf16[128,128,128]{2,1,0:T(8,128)(2,1)} %get-tuple-element.14), channel_id=1, replica_groups=mesh['row'=8,'col'=4] {'row','col'}, dimensions={0} | all-to-all | bytes 8388608 | tf_op jit(solution)/shard_map/all_to_all | solution.py:227
  383.1 20.6 %shard_map.90 = bf16[128,128,128]{2,1,0:T(8,128)(2,1)} custom-call(s32[256]{0:T(256)} %refs_0_.7, s32[256]{0:T(256)} %refs_1_.7, s32[128]{0:T(128)} %reshape.15.refs_2_.ids_ref, bf16[128,128,128]{2,1,0:T(8,128)(2,1)} %all_to_all.30.refs_3_, f32[16,128,128]{2,1,0:T(8,128)} %get-tuple-element.11.spam_ref.refs_4_.refs_3_, ...), custom_call_target="tpu_custom_call" | custom-call | tf_op jit(solution)/shard_map/pallas_call | solution.py:273
  403.7 97.0 %all_to_all.31.refs_2_ = bf16[128,128,128]{2,1,0:T(8,128)(2,1)} all-to-all(bf16[128,128,128]{2,1,0:T(8,128)(2,1)} %shard_map.90), channel_id=1, replica_groups=mesh['row'=8,'col'=4] {'row','col'}, dimensions={0} | all-to-all | bytes 8388608 | tf_op jit(solution)/shard_map/all_to_all | solution.py:227
  500.7 19.6 %shard_map.91 = f32[2048,128]{1,0:T(8,128)} custom-call(s32[256]{0:T(256)} %refs_0_.7, s32[256]{0:T(256)} %refs_1_.7, bf16[128,128,128]{2,1,0:T(8,128)(2,1)} %all_to_all.31.refs_2_, f32[16,128,128]{2,1,0:T(8,128)} %get-tuple-element.11.spam_ref.refs_4_.refs_3_, bf16[256,128,128]{2,1,0:T(8,128)(2,1)} %refs_4_.3), custom_call_target="tpu_custom_call" | custom-call | tf_op jit(solution)/shard_map/pallas_call | solution.py:282
Async XLA Ops:
  2.0 47.1 %all-to-all-start = ((s32[32,1,4]{2,1,0:T(1,128)}), s32[32,1,4]{2,1,0:T(1,128)S(1)}, u32[]{:S(2)}, u32[]{:S(2)}) async-start(s32[32,1,4]{2,1,0:T(1,128)} %bitcast), calls=%async_computation | async-start | bytes 32768 | tf_op jit(solution)/shard_map/all_to_all | solution.py:227
  49.1 100.6 %all-to-all-start.1 = ((s16[32,528,128]{2,1,0:T(8,128)(2,1)}), s16[32,528,128]{2,1,0:T(8,128)(2,1)}, u32[]{:S(2)}, u32[]{:S(2)}) async-start(s16[32,528,128]{2,1,0:T(8,128)(2,1)} %shard_map.87), calls=%async_computation.1 | async-start | bytes 8650752 | tf_op jit(solution)/shard_map/all_to_all | solution.py:227

commit v2 on v1

--- a/solution.py
+++ b/solution.py
@@ -13,6 +13,7 @@
 F32 = jnp.float32
 BF16 = jnp.bfloat16
 WORD = 15
+MESH = pl.DeviceIdType.MESH
 
 
 def seed_kernel(columns, good_seeds_ref, spam_cores_ref, good_ref, spam_ref):
@@ -141,22 +142,103 @@
         pack(first, cap, acc, out_ref)
 
 
-def shares(ids_ref, shield_ref, weight_ref, start_of, share, asked_ref):
+def shares(shield_ref, weight_ref, start_of, share_ref):
     def one(b, _):
-        share[b] = (shield_ref[b] * start_of(b) / weight_ref[b]).astype(BF16)
-        return 0
-
-    lax.fori_loop(0, share.shape[0], one, 0)
-
-    def ask(n, _):
-        asked_ref[n] = share[ids_ref[n]]
-        return 0
-
-    lax.fori_loop(0, asked_ref.shape[0], ask, 0)
+        share_ref[b] = (shield_ref[b] * start_of(b) / weight_ref[b]).astype(BF16)
+        return 0
+
+    lax.fori_loop(0, share_ref.shape[0], one, 0)
+
+
+def greet(devices):
+    barrier = pltpu.get_barrier_semaphore()
+    for device, there in devices:
+        @pl.when(there)
+        def _():
+            pl.semaphore_signal(barrier, inc=1, device_id=device, device_id_type=MESH)
+    pl.semaphore_wait(barrier, sum(jnp.where(there, 1, 0) for _, there in devices))
+
+
+def fetch_kernel(rows, columns, cap, want_ref, share_ref, fetched_ref, *scratch):
+    line = 2 * (columns - 1)
+    held, (picked, line_send, line_recv, send, recv) = scratch[:line], scratch[line:]
+    r, z = lax.axis_index("row"), lax.axis_index("col")
+    others = [lax.rem(r + d, rows) for d in range(1, rows)]
+    sides = (-1, 1)
+    inside = {side: (z + side >= 0) & (z + side < columns) for side in sides}
+    greet([((t, z), t >= 0) for t in others] + [((r, z + side), inside[side]) for side in sides])
+
+    def place(side, d):
+        return 2 * (d - 1) + (0 if side < 0 else 1)
+
+    def pass_on(source, d, side):
+        slot = place(-side, d)
+        return pltpu.make_async_remote_copy(
+            src_ref=source, dst_ref=held[slot],
+            send_sem=line_send.at[slot], recv_sem=line_recv.at[slot],
+            device_id=(r, z + side), device_id_type=MESH,
+        )
+
+    def serve(t, origin):
+        return pltpu.make_async_remote_copy(
+            src_ref=picked.at[t, pl.ds(origin * cap, cap)],
+            dst_ref=fetched_ref.at[pl.ds((r * columns + origin) * cap, cap)],
+            send_sem=send.at[t, origin], recv_sem=recv.at[r, origin],
+            device_id=(t, z), device_id_type=MESH,
+        )
+
+    def spread(source, origin):
+        before = None
+        for t in others:
+            for j in range(cap):
+                picked[t, origin * cap + j] = source[want_ref[t, origin * cap + j]]
+            if before is not None:
+                serve(before, origin).start()
+            before = t
+        for j in range(cap):
+            fetched_ref[(r * columns + origin) * cap + j] = source[want_ref[r, origin * cap + j]]
+        serve(before, origin).start()
+
+    for side in sides:
+        @pl.when(inside[side])
+        def _():
+            pass_on(share_ref, 1, side).start()
+    spread(share_ref, z)
+    for d in range(1, columns):
+        for side in sides:
+            origin = z + side * d
+
+            @pl.when((origin >= 0) & (origin < columns))
+            def _():
+                here = held[place(side, d)]
+                pass_on(share_ref, d, -side).wait_recv()
+
+                if d < columns - 1:
+                    @pl.when(inside[-side])
+                    def _():
+                        pass_on(here, d + 1, -side).start()
+
+                spread(here, origin)
+    for origin in range(columns):
+        for t in others:
+            serve(t, origin).wait_send()
+            pltpu.make_async_remote_copy(
+                src_ref=picked.at[t, pl.ds(origin * cap, cap)],
+                dst_ref=fetched_ref.at[pl.ds((t * columns + origin) * cap, cap)],
+                send_sem=send.at[t, origin], recv_sem=recv.at[t, origin],
+                device_id=(t, z), device_id_type=MESH,
+            ).wait_recv()
+    for d in range(columns - 1):
+        for side in sides:
+            origin = z - side * d
+
+            @pl.when((origin >= 0) & (origin < columns) & inside[side])
+            def _():
+                pass_on(share_ref, d + 1, side).wait_send()
 
 
 def trust_kernel(cap, ids_ref, arrived_ref, good_ref, spam_ref, weight_ref,
-                 trust_ref, shield_ref, asked_ref, inflow, share):
+                 trust_ref, shield_ref, share_ref, inflow):
     unpack(cap, ids_ref, arrived_ref, inflow, None)
     size = inflow.shape[2]
 
@@ -167,15 +249,15 @@
         return 0
 
     lax.fori_loop(0, inflow.shape[0], one, 0)
-    shares(ids_ref, shield_ref, weight_ref, lambda b: spam_ref[b], share, asked_ref)
+    shares(shield_ref, weight_ref, lambda b: spam_ref[b], share_ref)
 
 
 def pull_kernel(last, *refs):
     if last:
         src_ref, slot_ref, fetched_ref, spam_ref, tiles_ref, out_ref, acc = refs
     else:
-        (src_ref, slot_ref, ids_ref, fetched_ref, spam_ref, shield_ref, weight_ref, tiles_ref,
-         out_ref, acc, share) = refs
+        (src_ref, slot_ref, fetched_ref, spam_ref, shield_ref, weight_ref, tiles_ref,
+         out_ref, acc) = refs
     step = pl.program_id(0)
     per_step = tiles_ref.shape[0]
     size = acc.shape[2]
@@ -206,7 +288,7 @@
 
             lax.fori_loop(0, acc.shape[0], one, 0)
         else:
-            shares(ids_ref, shield_ref, weight_ref, distrust, share, out_ref)
+            shares(shield_ref, weight_ref, distrust, out_ref)
 
 
 def body(columns, tiles, tile_src, tile_slot, slot_block, out_degree, good_seeds, spam_cores):
@@ -227,6 +309,9 @@
         return lax.all_to_all(x, AXES, split_axis=0, concat_axis=0, tiled=True)
 
     ids = exchange(slot_block.reshape(peers, cap)).reshape(slots)
+    want = lax.all_to_all(
+        slot_block.reshape(peers // columns, columns * cap), "row", split_axis=0, concat_axis=0, tiled=True
+    )
     good, spam = pl.pallas_call(
         functools.partial(seed_kernel, columns),
         out_shape=(shape(vector, F32), shape(vector, F32)),
@@ -261,24 +346,39 @@
         ],
     )(tile_src, tile_slot, ids, arrived, good, degree, tiles)
     arrived = exchange(outgoing)
-    asked_shape = shape((slots, seeds, size), BF16)
-    trust, shield, asked = pl.pallas_call(
+    rows = peers // columns
+    fetch = pl.pallas_call(
+        functools.partial(fetch_kernel, rows, columns, cap),
+        out_shape=shape((slots, seeds, size), BF16),
+        in_specs=[SM, VM],
+        out_specs=VM,
+        scratch_shapes=[
+            *[pltpu.VMEM(vector, BF16)] * (2 * columns - 2),
+            pltpu.VMEM((rows, columns * cap, seeds, size), BF16),
+            pltpu.SemaphoreType.DMA((2 * columns - 2,)),
+            pltpu.SemaphoreType.DMA((2 * columns - 2,)),
+            pltpu.SemaphoreType.DMA((rows, columns)),
+            pltpu.SemaphoreType.DMA((rows, columns)),
+        ],
+        compiler_params=pltpu.CompilerParams(collective_id=0, has_side_effects=True),
+    )
+    trust, shield, share = pl.pallas_call(
         functools.partial(trust_kernel, cap),
-        out_shape=(shape((hosts, seeds), F32), shape(vector, F32), asked_shape),
+        out_shape=(shape((hosts, seeds), F32), shape(vector, F32), shape(vector, BF16)),
         in_specs=[SM, VM, VM, VM, VM],
         out_specs=(VM, VM, VM),
-        scratch_shapes=[pltpu.VMEM(vector, F32), pltpu.VMEM(vector, BF16)],
+        scratch_shapes=[pltpu.VMEM(vector, F32)],
     )(ids, arrived, good, spam, weight)
-    fetched = exchange(asked)
-    asked = pl.pallas_call(
+    fetched = fetch(want, share)
+    share = pl.pallas_call(
         functools.partial(pull_kernel, False),
         grid=(steps,),
-        out_shape=asked_shape,
-        in_specs=[SM, SM, SM, VM, VM, VM, VM, tile_spec],
+        out_shape=shape(vector, BF16),
+        in_specs=[SM, SM, VM, VM, VM, VM, tile_spec],
         out_specs=VM,
-        scratch_shapes=[pltpu.VMEM(vector, F32), pltpu.VMEM(vector, BF16)],
-    )(tile_src, tile_slot, ids, fetched, spam, shield, weight, tiles)
-    fetched = exchange(asked)
+        scratch_shapes=[pltpu.VMEM(vector, F32)],
+    )(tile_src, tile_slot, fetched, spam, shield, weight, tiles)
+    fetched = fetch(want, share)
     distrust = pl.pallas_call(
         functools.partial(pull_kernel, True),
         grid=(steps,),

time: 521 us -> 438 us (0.84)
  blocking collectives: 298 us -> 0 us
  Pallas kernels: 111 us -> 221 us
  waiting for transfers between devices: 92.8 us -> 187 us
  starting transfers between devices: 12.9 us -> 23.7 us
    all_to_all x3 -> x0, blocking collectives: 298 us -> none  [exchange(): return lax.all_to_all(x, AXES, split_axis=0, concat_axis=0, tiled=True)]
    pallas_call x0 -> x2, Pallas kernels: none -> 113 us  [body(): fetched = fetch(want, share)]
    all_to_all x2 -> x3, waiting for transfers between devices: 92.8 us -> 187 us  [exchange(): return lax.all_to_all(x, AXES, split_axis=0, concat_axis=0, tiled=True)]
    all_to_all x2 -> x3, starting transfers between devices: 12.9 us -> 19 us  [exchange(): return lax.all_to_all(x, AXES, split_axis=0, concat_axis=0, tiled=True)]
  transfers between devices with their start and end apart: 2 -> 4, of which waited for: 1 -> 2; matrix products, arithmetic and copies ran while one was open for 1% -> 1% of each run, Pallas kernels for 7% -> 11%
where the time goes in v2:
time: 438 us
  Pallas kernels  221 us (50%)
  waiting for transfers between devices  187 us (43%)
  starting transfers between devices  23.7 us (5%)
  local copies, waits for them, and re-layouts  5.33 us (1%)
    all_to_all x3, waiting for transfers between devices, exchange(): return lax.all_to_all(x, AXES, split_axis=0, concat_axis=0, tiled=True)  187 us
    pallas_call x2, Pallas kernels, body(): fetched = fetch(want, share)  113 us
    pallas_call x1, Pallas kernels, body(): pl.pallas_call(functools.partial(push_kernel, True, cap), grid=(steps,),...  23.2 us
    pallas_call x1, Pallas kernels, body(): pl.pallas_call(functools.partial(push_kernel, False, cap), grid=(steps,),...  22.8 us
    pallas_call x1, Pallas kernels, body(): pl.pallas_call(functools.partial(pull_kernel, True), grid=(steps,), out_s...  19.7 us
    all_to_all x3, starting transfers between devices, exchange(): return lax.all_to_all(x, AXES, split_axis=0, concat_axis=0, tiled=True)  19 us
    pallas_call x1, Pallas kernels, body(): pl.pallas_call(functools.partial(pull_kernel, False), grid=(steps,), out_...  18.6 us
    pallas_call x1, Pallas kernels, body(): pl.pallas_call(functools.partial(seed_kernel, columns), out_shape=(shape(...  15.3 us
  transfers between devices with their start and end apart: 4, of which 2 were waited for; matrix products, arithmetic and copies ran while one was open for 1% of the time, Pallas kernels for 11%

profile of v2, /device:TPU:1, one launch (start us, length us, event | category | flops | bytes accessed | tf_op | source)
XLA Modules:
  0.0 437.8 jit_solution(4947720079804638384)
XLA Ops:
  0.6 1.4 all_to_all.19
  2.0 7.1 %all-to-all-start = ((s32[32,1,4]{2,1,0:T(1,128)}), s32[32,1,4]{2,1,0:T(1,128)S(1)}, u32[]{:S(2)}, u32[]{:S(2)}) async-start(s32[32,1,4]{2,1,0:T(1,128)} %bitcast), calls=%async_computation | async-start | bytes 32768 | tf_op jit(solution)/shard_map/all_to_all | solution.py:309
  9.1 1.5 copy.12.spam_cores_ref
  10.6 15.3 %shard_map.86 = (f32[16,128,128]{2,1,0:T(8,128)}, f32[16,128,128]{2,1,0:T(8,128)}) custom-call(s32[128,128]{1,0:T(8,128)} %good_seeds_ref.1, s32[128,64]{1,0:T(8,128)} %copy.12.spam_cores_ref), custom_call_target="tpu_custom_call" | custom-call | tf_op jit(solution)/shard_map/pallas_call | solution.py:315
  25.9 23.2 %shard_map.87 = s16[32,528,128]{2,1,0:T(8,128)(2,1)} custom-call(s32[256]{0:T(256)} %refs_0_.7, s32[256]{0:T(256)} %refs_1_.7, f32[16,128,128]{2,1,0:T(8,128)} %get-tuple-element.9.refs_2_.refs_4_.good_ref, s32[16,1,128]{2,1,0:T(1,128)} %bitcast.6, bf16[256,128,128]{2,1,0:T(8,128)(2,1)} %refs_4_.3), custom_call_target="tpu_custom_call" | custom-call | tf_op jit(solution)/shard_map/pallas_call | solution.py:324
  49.1 0.0 all-to-all-done
  49.1 5.9 %all-to-all-start.1 = ((s16[32,528,128]{2,1,0:T(8,128)(2,1)}), s16[32,528,128]{2,1,0:T(8,128)(2,1)}, u32[]{:S(2)}, u32[]{:S(2)}) async-start(s16[32,528,128]{2,1,0:T(8,128)(2,1)} %shard_map.87), calls=%async_computation.1 | async-start | bytes 8650752 | tf_op jit(solution)/shard_map/all_to_all | solution.py:309
  55.0 0.5 broadcast.3
  55.5 0.7 reduce.3
  56.2 0.7 reshape.19.refs_2_.ids_ref
  56.9 92.8 %all-to-all-done.1.refs_3_ = s16[32,528,128]{2,1,0:T(8,128)(2,1)} async-done(((s16[32,528,128]{2,1,0:T(8,128)(2,1)}), s16[32,528,128]{2,1,0:T(8,128)(2,1)}, u32[]{:S(2)}, u32[]{:S(2)}) %all-to-all-start.1) | async-done | bytes 4325408 | tf_op jit(solution)/shard_map/all_to_all | solution.py:309
  149.8 22.8 %shard_map.88 = (s16[32,528,128]{2,1,0:T(8,128)(2,1)}, f32[16,1,128]{2,1,0:T(1,128)}) custom-call(s32[256]{0:T(256)} %refs_0_.7, s32[256]{0:T(256)} %refs_1_.7, s32[128]{0:T(128)} %reshape.19.refs_2_.ids_ref, s16[32,528,128]{2,1,0:T(8,128)(2,1)} %all-to-all-done.1.refs_3_, f32[16,128,128]{2,1,0:T(8,128)} %get-tuple-element.9.refs_2_.refs_4_.good_ref, ...), custom_call_target="tpu_custom_call" | custom-call | tf_op jit(solution)/shard_map/pallas_call | solution.py:336
  172.5 0.0 copy-start.1
  172.5 6.0 %all-to-all-start.2 = ((s16[32,528,128]{2,1,0:T(8,128)(2,1)}), s16[32,528,128]{2,1,0:T(8,128)(2,1)}, u32[]{:S(2)}, u32[]{:S(2)}) async-start(s16[32,528,128]{2,1,0:T(8,128)(2,1)} %get-tuple-element.10), calls=%async_computation.2 | async-start | bytes 8650752 | tf_op jit(solution)/shard_map/all_to_all | solution.py:309
  178.5 0.0 copy-done.1
  178.5 0.7 all_to_all.23
  179.2 94.1 %all-to-all-done.2.arrived_ref = s16[32,528,128]{2,1,0:T(8,128)(2,1)} async-done(((s16[32,528,128]{2,1,0:T(8,128)(2,1)}), s16[32,528,128]{2,1,0:T(8,128)(2,1)}, u32[]{:S(2)}, u32[]{:S(2)}) %all-to-all-start.2) | async-done | bytes 4325408 | tf_op jit(solution)/shard_map/all_to_all | solution.py:309
  273.2 4.7 %all-to-all-start.3 = ((s32[8,1,16]{2,1,0:T(1,128)}), s32[8,1,16]{2,1,0:T(1,128)S(1)}, u32[]{:S(2)}, u32[]{:S(2)}) async-start(s32[8,1,16]{2,1,0:T(1,128)} %bitcast.2), calls=%async_computation.3 | async-start | bytes 8192 | tf_op jit(solution)/shard_map/all_to_all | solution.py:312
  278.0 7.8 %shard_map.89 = (f32[2048,128]{1,0:T(8,128)}, f32[16,128,128]{2,1,0:T(8,128)}, bf16[16,128,128]{2,1,0:T(8,128)(2,1)}) custom-call(s32[128]{0:T(128)} %reshape.19.refs_2_.ids_ref, s16[32,528,128]{2,1,0:T(8,128)(2,1)} %all-to-all-done.2.arrived_ref, f32[16,128,128]{2,1,0:T(8,128)} %get-tuple-element.9.refs_2_.refs_4_.good_ref, ...), custom_call_target="tpu_custom_call" | custom-call | tf_op jit(solution)/shard_map/pallas_call | solution.py:365
  285.7 0.0 all-to-all-done.3
  285.8 0.0 copy-start
  285.8 0.6 copy-done
  286.3 57.2 %shard_map.90.refs_2_ = bf16[128,128,128]{2,1,0:T(8,128)(2,1)} custom-call(s32[8,16]{1,0:T(8,128)} %bitcast.4, bf16[16,128,128]{2,1,0:T(8,128)(2,1)} %get-tuple-element.14.share_ref), custom_call_target="tpu_custom_call" | custom-call | tf_op jit(solution)/shard_map/pallas_call | solution.py:372
  343.6 18.6 %shard_map.91.share_ref = bf16[16,128,128]{2,1,0:T(8,128)(2,1)} custom-call(s32[256]{0:T(256)} %refs_0_.7, s32[256]{0:T(256)} %refs_1_.7, bf16[128,128,128]{2,1,0:T(8,128)(2,1)} %shard_map.90.refs_2_, f32[16,128,128]{2,1,0:T(8,128)} %get-tuple-element.11.spam_ref.refs_3_, f32[16,128,128]{2,1,0:T(8,128)} %get-tuple-element.15.refs_4_, ...), custom_call_target="tpu_custom_call" | custom-call | tf_op jit(solution)/shard_map/pallas_call | solution.py:373
  362.1 56.0 %shard_map.92.refs_2_ = bf16[128,128,128]{2,1,0:T(8,128)(2,1)} custom-call(s32[8,16]{1,0:T(8,128)} %bitcast.5, bf16[16,128,128]{2,1,0:T(8,128)(2,1)} %shard_map.91.share_ref), custom_call_target="tpu_custom_call" | custom-call | tf_op jit(solution)/shard_map/pallas_call | solution.py:381
  418.1 19.7 %shard_map.93 = f32[2048,128]{1,0:T(8,128)} custom-call(s32[256]{0:T(256)} %refs_0_.7, s32[256]{0:T(256)} %refs_1_.7, bf16[128,128,128]{2,1,0:T(8,128)(2,1)} %shard_map.92.refs_2_, f32[16,128,128]{2,1,0:T(8,128)} %get-tuple-element.11.spam_ref.refs_3_, bf16[256,128,128]{2,1,0:T(8,128)(2,1)} %refs_4_.3), custom_call_target="tpu_custom_call" | custom-call | tf_op jit(solution)/shard_map/pallas_call | solution.py:382
Async XLA Ops:
  2.0 47.1 %all-to-all-start = ((s32[32,1,4]{2,1,0:T(1,128)}), s32[32,1,4]{2,1,0:T(1,128)S(1)}, u32[]{:S(2)}, u32[]{:S(2)}) async-start(s32[32,1,4]{2,1,0:T(1,128)} %bitcast), calls=%async_computation | async-start | bytes 32768 | tf_op jit(solution)/shard_map/all_to_all | solution.py:309
  49.1 100.7 %all-to-all-start.1 = ((s16[32,528,128]{2,1,0:T(8,128)(2,1)}), s16[32,528,128]{2,1,0:T(8,128)(2,1)}, u32[]{:S(2)}, u32[]{:S(2)}) async-start(s16[32,528,128]{2,1,0:T(8,128)(2,1)} %shard_map.87), calls=%async_computation.1 | async-start | bytes 8650752 | tf_op jit(solution)/shard_map/all_to_all | solution.py:309
  172.5 6.0 %copy-start.1 = (s32[128]{0:T(128)S(1)}, s32[128]{0:T(128)}, u32[]{:S(2)}) copy-start(s32[128]{0:T(128)} %param.10) | copy-start | bytes 1540
  172.5 100.7 %all-to-all-start.2 = ((s16[32,528,128]{2,1,0:T(8,128)(2,1)}), s16[32,528,128]{2,1,0:T(8,128)(2,1)}, u32[]{:S(2)}, u32[]{:S(2)}) async-start(s16[32,528,128]{2,1,0:T(8,128)(2,1)} %get-tuple-element.10), calls=%async_computation.2 | async-start | bytes 8650752 | tf_op jit(solution)/shard_map/all_to_all | solution.py:309
  273.2 12.5 %all-to-all-start.3 = ((s32[8,1,16]{2,1,0:T(1,128)}), s32[8,1,16]{2,1,0:T(1,128)S(1)}, u32[]{:S(2)}, u32[]{:S(2)}) async-start(s32[8,1,16]{2,1,0:T(1,128)} %bitcast.2), calls=%async_computation.3 | async-start | bytes 8192 | tf_op jit(solution)/shard_map/all_to_all | solution.py:312
  285.8 0.6 copy-start

commit v3 on v2

--- a/solution.py
+++ b/solution.py
@@ -80,34 +80,11 @@
     lax.fori_loop(0, peers, one, 0)
 
 
-def unpack(cap, ids_ref, arrived_ref, inflow, weight):
-    peers = arrived_ref.shape[0]
-    size = inflow.shape[2]
-    inflow[...] = jnp.zeros_like(inflow)
-    if weight is not None:
-        weight[...] = jnp.ones_like(weight)
-
-    def one(p, _):
-        rows = arrived_ref[p, cap * size :, :].astype(jnp.int32).astype(F32)
-        for c in range(cap):
-            b = ids_ref[p * cap + c]
-            value = arrived_ref[p, c * size : (c + 1) * size, :].astype(jnp.int32).astype(F32)
-            inflow[b] += value * jnp.exp2(rows[c : c + 1, :] - WORD)
-            if weight is not None:
-                at = cap + 3 * c
-                f, high, low = (rows[at + i : at + i + 1, :] for i in range(3))
-                weight[b] += (high + low * F32(2.0**-WORD)) * jnp.exp2(f - WORD)
-        return 0
-
-    lax.fori_loop(0, peers, one, 0)
-
-
 def push_kernel(first, cap, *refs):
     if first:
         src_ref, slot_ref, good_ref, degree_ref, tiles_ref, out_ref, acc, scaled = refs
     else:
-        (src_ref, slot_ref, ids_ref, arrived_ref, good_ref, degree_ref, tiles_ref,
-         out_ref, weight_ref, acc, scaled, inflow) = refs
+        src_ref, slot_ref, inflow, good_ref, degree_ref, tiles_ref, out_ref, acc, scaled = refs
     step = pl.program_id(0)
     blocks, seeds, size = good_ref.shape
     per_step = tiles_ref.shape[0]
@@ -115,9 +92,6 @@
     @pl.when(step == 0)
     def _():
         acc[...] = jnp.zeros_like(acc)
-        if not first:
-            unpack(cap, ids_ref, arrived_ref, inflow, weight_ref)
-
         def one(b, _):
             degree = degree_ref[b].astype(F32)
             trust = good_ref[b]
@@ -237,9 +211,140 @@
                 pass_on(share_ref, d + 1, side).wait_send()
 
 
-def trust_kernel(cap, ids_ref, arrived_ref, good_ref, spam_ref, weight_ref,
-                 trust_ref, shield_ref, share_ref, inflow):
-    unpack(cap, ids_ref, arrived_ref, inflow, None)
+def reduce_kernel(first, rows, columns, cap, want_ref, words_ref, *refs):
+    inflow_ref, refs = refs[0], refs[1:]
+    if first:
+        weight_ref, refs = refs[0], refs[1:]
+    (landed, table, partial, exps, scales, packed, final,
+     own, send, recv, line_send, line_recv) = refs
+    r, z = lax.axis_index("row"), lax.axis_index("col")
+    blocks, seeds, size = partial.shape
+    others = [lax.rem(r + d, rows) for d in range(1, rows)]
+    order = [columns // 2] + [d for d in range(1, columns) if d != columns // 2] + [0]
+    block_iota = lax.broadcasted_iota(jnp.int32, (blocks, size), 0)
+    data = blocks * seeds
+    greet(
+        [((t, z), t >= 0) for t in others]
+        + [((r, lax.rem(z + d, columns)), z >= 0) for d in range(1, columns)]
+    )
+
+    def across(d, t, origin):
+        return pltpu.make_async_remote_copy(
+            src_ref=words_ref.at[t * columns + lax.rem(z + d, columns)], dst_ref=landed.at[d, origin],
+            send_sem=send.at[d, t], recv_sem=recv.at[d, origin], device_id=(t, z), device_id_type=MESH,
+        )
+
+    def mine(d):
+        return pltpu.make_async_copy(
+            words_ref.at[r * columns + lax.rem(z + d, columns)], landed.at[d, r], own.at[d]
+        )
+
+    def along(d):
+        return pltpu.make_async_remote_copy(
+            src_ref=packed.at[d - 1], dst_ref=final.at[d - 1],
+            send_sem=line_send.at[d - 1], recv_sem=line_recv.at[d - 1],
+            device_id=(r, lax.rem(z + d, columns)), device_id_type=MESH,
+        )
+
+    def to_int16(value):
+        return value.astype(jnp.int32).astype(jnp.int16)
+
+    def to_float(value):
+        return value.astype(jnp.int32).astype(F32)
+
+    for d in order:
+        for t in others:
+            across(d, t, r).start()
+        mine(d).start()
+
+    cols = jnp.zeros((blocks, size), F32)
+    for d in order:
+        y = lax.rem(z + d, columns)
+        mine(d).wait()
+        for t in others:
+            across(d, t, t).wait_recv()
+
+        def weigh(q, cols):
+            tail = to_float(landed[d, q, cap * seeds :, :])
+            for c in range(cap):
+                hit = block_iota == want_ref[q, y * cap + c]
+                scale = jnp.exp2(tail[c : c + 1, :] - WORD)
+                table[q * cap + c] = jnp.where(hit, jnp.broadcast_to(scale, (blocks, size)), F32(0))
+                if first:
+                    f, high, low = (tail[cap + 3 * c + i : cap + 3 * c + i + 1, :] for i in range(3))
+                    col = (high + low * F32(2.0**-WORD)) * jnp.exp2(f - WORD)
+                    cols = cols + jnp.where(hit, jnp.broadcast_to(col, (blocks, size)), F32(0))
+            return cols
+
+        cols = lax.fori_loop(0, rows, weigh, jnp.zeros((blocks, size), F32))
+
+        def strip(i, _):
+            at = pl.multiple_of(i * 16, 16)
+
+            def add(q, sums):
+                sums = list(sums)
+                for c in range(cap):
+                    value = to_float(landed[d, q, pl.ds(pl.multiple_of(c * seeds + at, 16), 16), :])
+                    for b in range(blocks):
+                        sums[b] = sums[b] + value * table[q * cap + c, b : b + 1, :]
+                return tuple(sums)
+
+            sums = lax.fori_loop(0, rows, add, (jnp.zeros((16, size), F32),) * blocks)
+            for b in range(blocks):
+                partial[b, pl.ds(at, 16), :] = sums[b]
+            return 0
+
+        lax.fori_loop(0, seeds // 16, strip, 0)
+        if d:
+            def squeeze(b, _):
+                value = partial[b]
+                e = exponent_of(jnp.max(jnp.abs(value), axis=0, keepdims=True))
+                exps[pl.ds(b, 1), :] = e
+                packed[d - 1, pl.ds(pl.multiple_of(b * seeds, seeds), seeds), :] = to_int16(
+                    to_words(value * jnp.exp2(WORD - e))
+                )
+                return 0
+
+            lax.fori_loop(0, blocks, squeeze, 0)
+            packed[d - 1, data : data + blocks, :] = to_int16(exps[...])
+            if first:
+                f = exponent_of(jnp.abs(cols))
+                scaled = cols * jnp.exp2(WORD - f)
+                high = to_words(scaled)
+                for i, row in enumerate((f, high, to_words((scaled - high) * F32(2.0**WORD)))):
+                    packed[d - 1, data + (i + 1) * blocks : data + (i + 2) * blocks, :] = to_int16(row)
+            along(d).start()
+
+    for d in order[:-1]:
+        along(d).wait_recv()
+        scales[d - 1] = jnp.exp2(to_float(final[d - 1, data : data + blocks, :]) - WORD)
+        if first:
+            f, high, low = (
+                to_float(final[d - 1, data + (i + 1) * blocks : data + (i + 2) * blocks, :])
+                for i in range(3)
+            )
+            cols = cols + (high + low * F32(2.0**-WORD)) * jnp.exp2(f - WORD)
+    if first:
+        for b in range(blocks):
+            weight_ref[b] = F32(1) + cols[b : b + 1, :]
+
+    def finish(b, _):
+        total = partial[b]
+        for d in range(1, columns):
+            value = to_float(final[d - 1, pl.ds(pl.multiple_of(b * seeds, seeds), seeds), :])
+            total = total + value * scales[d - 1, pl.ds(b, 1), :]
+        inflow_ref[b] = total
+        return 0
+
+    lax.fori_loop(0, blocks, finish, 0)
+    for d in order:
+        for t in others:
+            across(d, t, r).wait_send()
+    for d in order[:-1]:
+        along(d).wait_send()
+
+
+def trust_kernel(inflow, good_ref, spam_ref, weight_ref, trust_ref, shield_ref, share_ref):
     size = inflow.shape[2]
 
     def one(b, _):
@@ -305,12 +410,9 @@
     vector = (blocks, seeds, size)
     degree = out_degree.reshape(blocks, 1, size)
 
-    def exchange(x):
-        return lax.all_to_all(x, AXES, split_axis=0, concat_axis=0, tiled=True)
-
-    ids = exchange(slot_block.reshape(peers, cap)).reshape(slots)
+    rows = peers // columns
     want = lax.all_to_all(
-        slot_block.reshape(peers // columns, columns * cap), "row", split_axis=0, concat_axis=0, tiled=True
+        slot_block.reshape(rows, columns * cap), "row", split_axis=0, concat_axis=0, tiled=True
     )
     good, spam = pl.pallas_call(
         functools.partial(seed_kernel, columns),
@@ -332,21 +434,46 @@
             pltpu.VMEM((blocks, seeds + 16, size), BF16),
         ],
     )(tile_src, tile_slot, good, degree, tiles)
-    arrived = exchange(outgoing)
-    outgoing, weight = pl.pallas_call(
+    def reduce(first, words_in):
+        long = blocks * seeds + blocks * (4 if first else 1)
+        outs = (shape(vector, F32), shape((blocks, 1, size), F32))
+        return pl.pallas_call(
+            functools.partial(reduce_kernel, first, rows, columns, cap),
+            out_shape=outs if first else outs[:1],
+            in_specs=[SM, VM],
+            out_specs=(VM, VM) if first else (VM,),
+            scratch_shapes=[
+                pltpu.VMEM((columns, rows, cap * size + tail, size), jnp.int16),
+                pltpu.VMEM((rows * cap, blocks, size), F32),
+                pltpu.VMEM(vector, F32),
+                pltpu.VMEM((blocks, size), F32),
+                pltpu.VMEM((columns - 1, blocks, size), F32),
+                pltpu.VMEM((columns - 1, long, size), jnp.int16),
+                pltpu.VMEM((columns - 1, long, size), jnp.int16),
+                pltpu.SemaphoreType.DMA((columns,)),
+                pltpu.SemaphoreType.DMA((columns, rows)),
+                pltpu.SemaphoreType.DMA((columns, rows)),
+                pltpu.SemaphoreType.DMA((columns - 1,)),
+                pltpu.SemaphoreType.DMA((columns - 1,)),
+            ],
+            compiler_params=pltpu.CompilerParams(
+                collective_id=1 if first else 2, has_side_effects=True
+            ),
+        )(want, words_in)
+
+    inflow, weight = reduce(True, outgoing)
+    outgoing = pl.pallas_call(
         functools.partial(push_kernel, False, cap),
         grid=(steps,),
-        out_shape=(words, shape((blocks, 1, size), F32)),
-        in_specs=[SM, SM, SM, VM, VM, VM, tile_spec],
-        out_specs=(VM, VM),
+        out_shape=words,
+        in_specs=[SM, SM, VM, VM, VM, tile_spec],
+        out_specs=VM,
         scratch_shapes=[
             pltpu.VMEM((slots, seeds, size), F32),
             pltpu.VMEM(vector, BF16),
-            pltpu.VMEM(vector, F32),
         ],
-    )(tile_src, tile_slot, ids, arrived, good, degree, tiles)
-    arrived = exchange(outgoing)
-    rows = peers // columns
+    )(tile_src, tile_slot, inflow, good, degree, tiles)
+    (inflow,) = reduce(False, outgoing)
     fetch = pl.pallas_call(
         functools.partial(fetch_kernel, rows, columns, cap),
         out_shape=shape((slots, seeds, size), BF16),
@@ -363,12 +490,11 @@
         compiler_params=pltpu.CompilerParams(collective_id=0, has_side_effects=True),
     )
     trust, shield, share = pl.pallas_call(
-        functools.partial(trust_kernel, cap),
+        trust_kernel,
         out_shape=(shape((hosts, seeds), F32), shape(vector, F32), shape(vector, BF16)),
-        in_specs=[SM, VM, VM, VM, VM],
+        in_specs=[VM, VM, VM, VM],
         out_specs=(VM, VM, VM),
-        scratch_shapes=[pltpu.VMEM(vector, F32)],
-    )(ids, arrived, good, spam, weight)
+    )(inflow, good, spam, weight)
     fetched = fetch(want, share)
     share = pl.pallas_call(
         functools.partial(pull_kernel, False),

time: 438 us -> 365 us (0.83)
  waiting for transfers between devices: 187 us -> 0.01 us
  Pallas kernels: 221 us -> 356 us
  starting transfers between devices: 23.7 us -> 5.21 us
    all_to_all x4 -> x1, waiting for transfers between devices: 187 us -> 0.01 us  [body(): lax.all_to_all(slot_block.reshape(rows, columns * cap), 'row', split_axis...]
    pallas_call x1 -> x3, Pallas kernels: 7.77 us -> 148 us  [the longest x2 143 us: reduce(): pl.pallas_call(functools.partial(reduce_kernel, first, rows, columns, cap...]
    all_to_all x4 -> x1, starting transfers between devices: 23.7 us -> 5.21 us  [body(): lax.all_to_all(slot_block.reshape(rows, columns * cap), 'row', split_axis...]
  transfers between devices with their start and end apart: 4 -> 1, of which waited for: 2 -> 0; matrix products, arithmetic and copies ran while one was open for 1% -> 0% of each run, Pallas kernels for 11% -> 11%
where the time goes in v3:
time: 365 us
  Pallas kernels  356 us (98%)
  starting transfers between devices  5.21 us (1%)
    pallas_call x2, Pallas kernels, reduce(): pl.pallas_call(functools.partial(reduce_kernel, first, rows, columns, cap...  143 us
    pallas_call x2, Pallas kernels, body(): fetched = fetch(want, share)  111 us
    pallas_call x1, Pallas kernels, body(): pl.pallas_call(functools.partial(push_kernel, True, cap), grid=(steps,),...  23.1 us
    pallas_call x1, Pallas kernels, body(): pl.pallas_call(functools.partial(push_kernel, False, cap), grid=(steps,),...  19.9 us
    pallas_call x1, Pallas kernels, body(): pl.pallas_call(functools.partial(pull_kernel, True), grid=(steps,), out_s...  19.7 us
    pallas_call x1, Pallas kernels, body(): pl.pallas_call(functools.partial(pull_kernel, False), grid=(steps,), out_...  18.6 us
    pallas_call x1, Pallas kernels, body(): pl.pallas_call(functools.partial(seed_kernel, columns), out_shape=(shape(...  15.2 us
  transfers between devices with their start and end apart: 1, of which 0 were waited for; matrix products, arithmetic and copies ran while one was open for 0% of the time, Pallas kernels for 11%

profile of v3, /device:TPU:1, one launch (start us, length us, event | category | flops | bytes accessed | tf_op | source)
XLA Modules:
  0.0 364.8 jit_solution(8049394273836880240)
XLA Ops:
  0.6 1.3 all_to_all.7
  2.0 5.2 %all-to-all-start = ((s32[8,1,16]{2,1,0:T(1,128)}), s32[8,1,16]{2,1,0:T(1,128)S(1)}, u32[]{:S(2)}, u32[]{:S(2)}) async-start(s32[8,1,16]{2,1,0:T(1,128)} %bitcast), calls=%async_computation | async-start | bytes 8192 | tf_op jit(solution)/shard_map/all_to_all | solution.py:414
  7.2 1.5 copy.11.spam_cores_ref
  8.7 15.2 %shard_map.86 = (f32[16,128,128]{2,1,0:T(8,128)}, f32[16,128,128]{2,1,0:T(8,128)}) custom-call(s32[128,128]{1,0:T(8,128)} %good_seeds_ref.1, s32[128,64]{1,0:T(8,128)} %copy.11.spam_cores_ref), custom_call_target="tpu_custom_call" | custom-call | tf_op jit(solution)/shard_map/pallas_call | solution.py:417
  23.9 23.1 %shard_map.87.words_ref = s16[32,528,128]{2,1,0:T(8,128)(2,1)} custom-call(s32[256]{0:T(256)} %refs_0_.7, s32[256]{0:T(256)} %refs_1_.7, f32[16,128,128]{2,1,0:T(8,128)} %get-tuple-element.9.refs_2_.refs_3_.good_ref, s32[16,1,128]{2,1,0:T(1,128)} %bitcast.7, bf16[256,128,128]{2,1,0:T(8,128)(2,1)} %refs_4_.3), custom_call_target="tpu_custom_call" | custom-call | tf_op jit(solution)/shard_map/pallas_call | solution.py:426
  47.0 0.0 all-to-all-done
  47.0 0.0 copy-start
  47.0 0.6 copy-done
  47.6 72.6 %shard_map.88 = (f32[16,128,128]{2,1,0:T(8,128)}, f32[16,1,128]{2,1,0:T(1,128)}) custom-call(s32[8,16]{1,0:T(8,128)} %bitcast.3, s16[32,528,128]{2,1,0:T(8,128)(2,1)} %shard_map.87.words_ref), custom_call_target="tpu_custom_call" | custom-call | tf_op jit(solution)/shard_map/pallas_call | solution.py:440
  120.2 19.9 %shard_map.89.words_ref = s16[32,528,128]{2,1,0:T(8,128)(2,1)} custom-call(s32[256]{0:T(256)} %refs_0_.7, s32[256]{0:T(256)} %refs_1_.7, f32[16,128,128]{2,1,0:T(8,128)} %get-tuple-element.10.refs_2_, f32[16,128,128]{2,1,0:T(8,128)} %get-tuple-element.9.refs_2_.refs_3_.good_ref, s32[16,1,128]{2,1,0:T(1,128)} %bitcast.8, bf16[256,128,128]{2,1,0:T(8,128)(2,1)} %refs_4_.3), custom_call_target="tpu_custom_call" | custom-call | tf_op jit(solution)/shard_map/pallas_call | solution.py:465
  140.1 70.0 %shard_map.90.inflow = f32[16,128,128]{2,1,0:T(8,128)} custom-call(s32[8,16]{1,0:T(8,128)} %bitcast.4, s16[32,528,128]{2,1,0:T(8,128)(2,1)} %shard_map.89.words_ref), custom_call_target="tpu_custom_call" | custom-call | tf_op jit(solution)/shard_map/pallas_call | solution.py:440
  210.1 5.3 %shard_map.91 = (f32[2048,128]{1,0:T(8,128)}, f32[16,128,128]{2,1,0:T(8,128)}, bf16[16,128,128]{2,1,0:T(8,128)(2,1)}) custom-call(f32[16,128,128]{2,1,0:T(8,128)} %shard_map.90.inflow, f32[16,128,128]{2,1,0:T(8,128)} %get-tuple-element.9.refs_2_.refs_3_.good_ref, f32[16,128,128]{2,1,0:T(8,128)} %get-tuple-element.11.spam_ref.refs_3_, ...), custom_call_target="tpu_custom_call" | custom-call | tf_op jit(solution)/shard_map/pallas_call | solution.py:492
  215.4 54.8 %shard_map.92.refs_2_ = bf16[128,128,128]{2,1,0:T(8,128)(2,1)} custom-call(s32[8,16]{1,0:T(8,128)} %bitcast.5, bf16[16,128,128]{2,1,0:T(8,128)(2,1)} %get-tuple-element.14.share_ref), custom_call_target="tpu_custom_call" | custom-call | tf_op jit(solution)/shard_map/pallas_call | solution.py:498
  270.2 18.6 %shard_map.93.share_ref = bf16[16,128,128]{2,1,0:T(8,128)(2,1)} custom-call(s32[256]{0:T(256)} %refs_0_.7, s32[256]{0:T(256)} %refs_1_.7, bf16[128,128,128]{2,1,0:T(8,128)(2,1)} %shard_map.92.refs_2_, f32[16,128,128]{2,1,0:T(8,128)} %get-tuple-element.11.spam_ref.refs_3_, f32[16,128,128]{2,1,0:T(8,128)} %get-tuple-element.15.refs_4_, ...), custom_call_target="tpu_custom_call" | custom-call | tf_op jit(solution)/shard_map/pallas_call | solution.py:499
  288.8 56.3 %shard_map.94.refs_2_ = bf16[128,128,128]{2,1,0:T(8,128)(2,1)} custom-call(s32[8,16]{1,0:T(8,128)} %bitcast.6, bf16[16,128,128]{2,1,0:T(8,128)(2,1)} %shard_map.93.share_ref), custom_call_target="tpu_custom_call" | custom-call | tf_op jit(solution)/shard_map/pallas_call | solution.py:507
  345.1 19.7 %shard_map.95 = f32[2048,128]{1,0:T(8,128)} custom-call(s32[256]{0:T(256)} %refs_0_.7, s32[256]{0:T(256)} %refs_1_.7, bf16[128,128,128]{2,1,0:T(8,128)(2,1)} %shard_map.94.refs_2_, f32[16,128,128]{2,1,0:T(8,128)} %get-tuple-element.11.spam_ref.refs_3_, bf16[256,128,128]{2,1,0:T(8,128)(2,1)} %refs_4_.3), custom_call_target="tpu_custom_call" | custom-call | tf_op jit(solution)/shard_map/pallas_call | solution.py:508
Async XLA Ops:
  2.0 45.1 %all-to-all-start = ((s32[8,1,16]{2,1,0:T(1,128)}), s32[8,1,16]{2,1,0:T(1,128)S(1)}, u32[]{:S(2)}, u32[]{:S(2)}) async-start(s32[8,1,16]{2,1,0:T(1,128)} %bitcast), calls=%async_computation | async-start | bytes 8192 | tf_op jit(solution)/shard_map/all_to_all | solution.py:414
  47.0 0.6 copy-start

commit v4 on v3

--- a/solution.py
+++ b/solution.py
@@ -13,33 +13,33 @@
 F32 = jnp.float32
 BF16 = jnp.bfloat16
 WORD = 15
+GROUP = 4
 MESH = pl.DeviceIdType.MESH
 
 
-def seed_kernel(columns, good_seeds_ref, spam_cores_ref, good_ref, spam_ref):
-    blocks, seeds, size = good_ref.shape
+def count_seeds(columns, source, target):
+    blocks, seeds, size = target.shape
     hosts = blocks * size
     base = (lax.axis_index("row") * columns + lax.axis_index("col")) * hosts
-    for source, target in ((good_seeds_ref, good_ref), (spam_cores_ref, spam_ref)):
-        count = source.shape[1]
-        factor = F32(hosts / count)
-        block_iota = lax.broadcasted_iota(jnp.int32, (blocks, count), 0) * size
-        lane_iota = lax.broadcasted_iota(jnp.int32, (size, count), 0)
-
-        def one(s, _):
-            local = source[pl.ds(s, 1), :] - base
-            shifted = local - block_iota
-            inside = jnp.where((shifted >= 0) & (shifted < size), F32(1), F32(0)).astype(BF16)
-            start = jnp.max(jnp.where(local >= block_iota, block_iota, 0), axis=0, keepdims=True)
-            lane = jnp.where(lane_iota == local - start, F32(1), F32(0)).astype(BF16)
-            counts = lax.dot_general(
-                inside, lane, (((1,), (1,)), ((), ())), preferred_element_type=F32
-            )
-            for b in range(blocks):
-                target[b, pl.ds(s, 1), :] = counts[b : b + 1, :] * factor
-            return 0
-
-        lax.fori_loop(0, seeds, one, 0, unroll=4)
+    count = source.shape[1]
+    factor = F32(hosts / count)
+    block_iota = lax.broadcasted_iota(jnp.int32, (blocks, count), 0) * size
+    lane_iota = lax.broadcasted_iota(jnp.int32, (size, count), 0)
+
+    def one(s, _):
+        local = source[pl.ds(s, 1), :] - base
+        shifted = local - block_iota
+        inside = jnp.where((shifted >= 0) & (shifted < size), F32(1), F32(0)).astype(BF16)
+        start = jnp.max(jnp.where(local >= block_iota, block_iota, 0), axis=0, keepdims=True)
+        lane = jnp.where(lane_iota == local - start, F32(1), F32(0)).astype(BF16)
+        counts = lax.dot_general(
+            inside, lane, (((1,), (1,)), ((), ())), preferred_element_type=F32
+        )
+        for b in range(blocks):
+            target[b, pl.ds(s, 1), :] = counts[b : b + 1, :] * factor
+        return 0
+
+    lax.fori_loop(0, seeds, one, 0, unroll=4)
 
 
 def exponent_of(peak):
@@ -104,12 +104,18 @@
 
         lax.fori_loop(0, blocks, one, 0)
 
-    def one(k, _):
-        n = step * per_step + k
-        acc[slot_ref[n]] += jnp.dot(scaled[src_ref[n]], tiles_ref[k], preferred_element_type=F32)
-        return 0
-
-    lax.fori_loop(0, per_step, one, 0, unroll=4)
+    def some(g, _):
+        products = []
+        for k in range(GROUP):
+            n = step * per_step + g * GROUP + k
+            products.append(
+                jnp.dot(scaled[src_ref[n]], tiles_ref[g * GROUP + k], preferred_element_type=F32)
+            )
+        for k in range(GROUP):
+            acc[slot_ref[step * per_step + g * GROUP + k]] += products[k]
+        return 0
+
+    lax.fori_loop(0, per_step // GROUP, some, 0)
 
     @pl.when(step == pl.num_programs(0) - 1)
     def _():
@@ -212,9 +218,10 @@
 
 
 def reduce_kernel(first, rows, columns, cap, want_ref, words_ref, *refs):
-    inflow_ref, refs = refs[0], refs[1:]
     if first:
-        weight_ref, refs = refs[0], refs[1:]
+        cores_ref, inflow_ref, weight_ref, spam_ref, *refs = refs
+    else:
+        inflow_ref, *refs = refs
     (landed, table, partial, exps, scales, packed, final,
      own, send, recv, line_send, line_recv) = refs
     r, z = lax.axis_index("row"), lax.axis_index("col")
@@ -256,6 +263,8 @@
         for t in others:
             across(d, t, r).start()
         mine(d).start()
+    if first:
+        count_seeds(columns, cores_ref, spam_ref)
 
     cols = jnp.zeros((blocks, size), F32)
     for d in order:
@@ -371,15 +380,21 @@
     def _():
         acc[...] = jnp.zeros_like(acc)
 
-    def one(k, _):
-        n = step * per_step + k
-        acc[src_ref[n]] += lax.dot_general(
-            fetched_ref[slot_ref[n]], tiles_ref[k], (((1,), (1,)), ((), ())),
-            preferred_element_type=F32,
-        )
-        return 0
-
-    lax.fori_loop(0, per_step, one, 0, unroll=4)
+    def some(g, _):
+        products = []
+        for k in range(GROUP):
+            n = step * per_step + g * GROUP + k
+            products.append(
+                lax.dot_general(
+                    fetched_ref[slot_ref[n]], tiles_ref[g * GROUP + k], (((1,), (1,)), ((), ())),
+                    preferred_element_type=F32,
+                )
+            )
+        for k in range(GROUP):
+            acc[src_ref[step * per_step + g * GROUP + k]] += products[k]
+        return 0
+
+    lax.fori_loop(0, per_step // GROUP, some, 0)
 
     @pl.when(step == pl.num_programs(0) - 1)
     def _():
@@ -414,12 +429,12 @@
     want = lax.all_to_all(
         slot_block.reshape(rows, columns * cap), "row", split_axis=0, concat_axis=0, tiled=True
     )
-    good, spam = pl.pallas_call(
-        functools.partial(seed_kernel, columns),
-        out_shape=(shape(vector, F32), shape(vector, F32)),
-        in_specs=[VM, VM],
-        out_specs=(VM, VM),
-    )(good_seeds, spam_cores)
+    good = pl.pallas_call(
+        functools.partial(count_seeds, columns),
+        out_shape=shape(vector, F32),
+        in_specs=[VM],
+        out_specs=VM,
+    )(good_seeds)
 
     tile_spec = pl.BlockSpec((tile_count // steps, size, size), lambda i: (i, 0, 0))
     words = shape((peers, cap * size + tail, size), jnp.int16)
@@ -434,14 +449,14 @@
             pltpu.VMEM((blocks, seeds + 16, size), BF16),
         ],
     )(tile_src, tile_slot, good, degree, tiles)
-    def reduce(first, words_in):
+    def reduce(first, words_in, *rest):
         long = blocks * seeds + blocks * (4 if first else 1)
-        outs = (shape(vector, F32), shape((blocks, 1, size), F32))
+        outs = (shape(vector, F32), shape((blocks, 1, size), F32), shape(vector, F32))
         return pl.pallas_call(
             functools.partial(reduce_kernel, first, rows, columns, cap),
             out_shape=outs if first else outs[:1],
-            in_specs=[SM, VM],
-            out_specs=(VM, VM) if first else (VM,),
+            in_specs=[SM, VM, VM] if first else [SM, VM],
+            out_specs=(VM, VM, VM) if first else (VM,),
             scratch_shapes=[
                 pltpu.VMEM((columns, rows, cap * size + tail, size), jnp.int16),
                 pltpu.VMEM((rows * cap, blocks, size), F32),
@@ -459,9 +474,9 @@
             compiler_params=pltpu.CompilerParams(
                 collective_id=1 if first else 2, has_side_effects=True
             ),
-        )(want, words_in)
-
-    inflow, weight = reduce(True, outgoing)
+        )(want, words_in, *rest)
+
+    inflow, weight, spam = reduce(True, outgoing, spam_cores)
     outgoing = pl.pallas_call(
         functools.partial(push_kernel, False, cap),
         grid=(steps,),

time: 365 us -> 358 us (0.981)
  Pallas kernels: 356 us -> 349 us
    pallas_call x1, Pallas kernels: 15.2 us -> 8.41 us  [body(): pl.pallas_call(functools.partial(count_seeds, columns), out_shape=shape(v...]
  transfers between devices with their start and end apart: 1 -> 1, of which waited for: 0 -> 0; matrix products, arithmetic and copies ran while one was open for 0% -> 0% of each run, Pallas kernels for 11% -> 9%
where the time goes in v4:
time: 358 us
  Pallas kernels  349 us (97%)
  starting transfers between devices  5.21 us (1%)
    pallas_call x2, Pallas kernels, reduce(): pl.pallas_call(functools.partial(reduce_kernel, first, rows, columns, cap...  143 us
    pallas_call x2, Pallas kernels, body(): fetched = fetch(want, share)  111 us
    pallas_call x1, Pallas kernels, body(): pl.pallas_call(functools.partial(push_kernel, True, cap), grid=(steps,),...  23 us
    pallas_call x1, Pallas kernels, body(): pl.pallas_call(functools.partial(push_kernel, False, cap), grid=(steps,),...  19.8 us
    pallas_call x1, Pallas kernels, body(): pl.pallas_call(functools.partial(pull_kernel, True), grid=(steps,), out_s...  19.7 us
    pallas_call x1, Pallas kernels, body(): pl.pallas_call(functools.partial(pull_kernel, False), grid=(steps,), out_...  18.6 us
    pallas_call x1, Pallas kernels, body(): pl.pallas_call(functools.partial(count_seeds, columns), out_shape=shape(v...  8.41 us
  transfers between devices with their start and end apart: 1, of which 0 were waited for; matrix products, arithmetic and copies ran while one was open for 0% of the time, Pallas kernels for 9%

profile of v4, /device:TPU:1, one launch (start us, length us, event | category | flops | bytes accessed | tf_op | source)
XLA Modules:
  0.0 358.0 jit_solution(11969209179598991087)
XLA Ops:
  0.6 1.3 all_to_all.7
  2.0 5.2 %all-to-all-start = ((s32[8,1,16]{2,1,0:T(1,128)}), s32[8,1,16]{2,1,0:T(1,128)S(1)}, u32[]{:S(2)}, u32[]{:S(2)}) async-start(s32[8,1,16]{2,1,0:T(1,128)} %bitcast), calls=%async_computation | async-start | bytes 8192 | tf_op jit(solution)/shard_map/all_to_all | solution.py:429
  7.2 1.5 copy.11.refs_0_
  8.7 8.4 %shard_map.86.refs_2_.refs_3_.good_ref = f32[16,128,128]{2,1,0:T(8,128)} custom-call(s32[128,128]{1,0:T(8,128)} %source.1), custom_call_target="tpu_custom_call" | custom-call | tf_op jit(solution)/shard_map/pallas_call | solution.py:432
  17.1 23.0 %shard_map.87.words_ref = s16[32,528,128]{2,1,0:T(8,128)(2,1)} custom-call(s32[256]{0:T(256)} %refs_0_.8, s32[256]{0:T(256)} %refs_1_.7, f32[16,128,128]{2,1,0:T(8,128)} %shard_map.86.refs_2_.refs_3_.good_ref, s32[16,1,128]{2,1,0:T(1,128)} %bitcast.7, bf16[256,128,128]{2,1,0:T(8,128)(2,1)} %refs_4_.3), custom_call_target="tpu_custom_call" | custom-call | tf_op jit(solution)/shard_map/pallas_call | solution.py:441
  40.1 0.0 all-to-all-done
  40.1 0.0 copy-start
  40.1 0.6 copy-done
  40.6 72.9 %shard_map.88 = (f32[16,128,128]{2,1,0:T(8,128)}, f32[16,1,128]{2,1,0:T(1,128)}, f32[16,128,128]{2,1,0:T(8,128)}) custom-call(s32[8,16]{1,0:T(8,128)} %bitcast.3, s16[32,528,128]{2,1,0:T(8,128)(2,1)} %shard_map.87.words_ref, s32[128,64]{1,0:T(8,128)} %copy.11.refs_0_), custom_call_target="tpu_custom_call" | custom-call | tf_op jit(solution)/shard_map/pallas_call | solution.py:455
  113.5 19.8 %shard_map.89.words_ref = s16[32,528,128]{2,1,0:T(8,128)(2,1)} custom-call(s32[256]{0:T(256)} %refs_0_.8, s32[256]{0:T(256)} %refs_1_.7, f32[16,128,128]{2,1,0:T(8,128)} %get-tuple-element.8.refs_2_, f32[16,128,128]{2,1,0:T(8,128)} %shard_map.86.refs_2_.refs_3_.good_ref, s32[16,1,128]{2,1,0:T(1,128)} %bitcast.8, bf16[256,128,128]{2,1,0:T(8,128)(2,1)} %refs_4_.3), custom_call_target="tpu_custom_call" | custom-call | tf_op jit(solution)/shard_map/pallas_call | solution.py:480
  133.4 70.0 %shard_map.90.inflow = f32[16,128,128]{2,1,0:T(8,128)} custom-call(s32[8,16]{1,0:T(8,128)} %bitcast.4, s16[32,528,128]{2,1,0:T(8,128)(2,1)} %shard_map.89.words_ref), custom_call_target="tpu_custom_call" | custom-call | tf_op jit(solution)/shard_map/pallas_call | solution.py:455
  203.4 5.3 %shard_map.91 = (f32[2048,128]{1,0:T(8,128)}, f32[16,128,128]{2,1,0:T(8,128)}, bf16[16,128,128]{2,1,0:T(8,128)(2,1)}) custom-call(f32[16,128,128]{2,1,0:T(8,128)} %shard_map.90.inflow, f32[16,128,128]{2,1,0:T(8,128)} %shard_map.86.refs_2_.refs_3_.good_ref, f32[16,128,128]{2,1,0:T(8,128)} %get-tuple-element.9.spam_ref.refs_3_, ...), custom_call_target="tpu_custom_call" | custom-call | tf_op jit(solution)/shard_map/pallas_call | solution.py:507
  208.7 54.8 %shard_map.92.refs_2_ = bf16[128,128,128]{2,1,0:T(8,128)(2,1)} custom-call(s32[8,16]{1,0:T(8,128)} %bitcast.5, bf16[16,128,128]{2,1,0:T(8,128)(2,1)} %get-tuple-element.12.share_ref), custom_call_target="tpu_custom_call" | custom-call | tf_op jit(solution)/shard_map/pallas_call | solution.py:513
  263.5 18.6 %shard_map.93.share_ref = bf16[16,128,128]{2,1,0:T(8,128)(2,1)} custom-call(s32[256]{0:T(256)} %refs_0_.8, s32[256]{0:T(256)} %refs_1_.7, bf16[128,128,128]{2,1,0:T(8,128)(2,1)} %shard_map.92.refs_2_, f32[16,128,128]{2,1,0:T(8,128)} %get-tuple-element.9.spam_ref.refs_3_, f32[16,128,128]{2,1,0:T(8,128)} %get-tuple-element.13.refs_4_, ...), custom_call_target="tpu_custom_call" | custom-call | tf_op jit(solution)/shard_map/pallas_call | solution.py:514
  282.1 56.2 %shard_map.94.refs_2_ = bf16[128,128,128]{2,1,0:T(8,128)(2,1)} custom-call(s32[8,16]{1,0:T(8,128)} %bitcast.6, bf16[16,128,128]{2,1,0:T(8,128)(2,1)} %shard_map.93.share_ref), custom_call_target="tpu_custom_call" | custom-call | tf_op jit(solution)/shard_map/pallas_call | solution.py:522
  338.3 19.7 %shard_map.95 = f32[2048,128]{1,0:T(8,128)} custom-call(s32[256]{0:T(256)} %refs_0_.8, s32[256]{0:T(256)} %refs_1_.7, bf16[128,128,128]{2,1,0:T(8,128)(2,1)} %shard_map.94.refs_2_, f32[16,128,128]{2,1,0:T(8,128)} %get-tuple-element.9.spam_ref.refs_3_, bf16[256,128,128]{2,1,0:T(8,128)(2,1)} %refs_4_.3), custom_call_target="tpu_custom_call" | custom-call | tf_op jit(solution)/shard_map/pallas_call | solution.py:523
Async XLA Ops:
  2.0 38.1 %all-to-all-start = ((s32[8,1,16]{2,1,0:T(1,128)}), s32[8,1,16]{2,1,0:T(1,128)S(1)}, u32[]{:S(2)}, u32[]{:S(2)}) async-start(s32[8,1,16]{2,1,0:T(1,128)} %bitcast), calls=%async_computation | async-start | bytes 8192 | tf_op jit(solution)/shard_map/all_to_all | solution.py:429
  40.1 0.6 copy-start

commit v5 on v4

--- a/solution.py
+++ b/solution.py
@@ -13,7 +13,7 @@
 F32 = jnp.float32
 BF16 = jnp.bfloat16
 WORD = 15
-GROUP = 4
+GROUP = 16
 MESH = pl.DeviceIdType.MESH
 
 

time: 358 us -> 337 us (0.941)
  Pallas kernels: 349 us -> 327 us
    pallas_call x1, Pallas kernels: 23 us -> 16.5 us  [body(): pl.pallas_call(functools.partial(push_kernel, True, cap), grid=(steps,),...]
    pallas_call x1, Pallas kernels: 18.6 us -> 13.2 us  [body(): pl.pallas_call(functools.partial(pull_kernel, False), grid=(steps,), out_...]
    pallas_call x1, Pallas kernels: 19.7 us -> 14.4 us  [body(): pl.pallas_call(functools.partial(pull_kernel, True), grid=(steps,), out_s...]
    pallas_call x1, Pallas kernels: 19.8 us -> 15.1 us  [body(): pl.pallas_call(functools.partial(push_kernel, False, cap), grid=(steps,),...]
  transfers between devices with their start and end apart: 1 -> 1, of which waited for: 0 -> 0; matrix products, arithmetic and copies ran while one was open for 0% -> 0% of each run, Pallas kernels for 9% -> 7%
where the time goes in v5:
time: 337 us; the launch traced here: 336 us
  Pallas kernels  327 us (97%)
  starting transfers between devices  5.21 us (2%)
  local copies, waits for them, and re-layouts  3.41 us (1%)
    pallas_call x2, Pallas kernels, reduce(): pl.pallas_call(functools.partial(reduce_kernel, first, rows, columns, cap...  143 us
    pallas_call x2, Pallas kernels, body(): fetched = fetch(want, share)  111 us
    pallas_call x1, Pallas kernels, body(): pl.pallas_call(functools.partial(push_kernel, True, cap), grid=(steps,),...  16.5 us
    pallas_call x1, Pallas kernels, body(): pl.pallas_call(functools.partial(push_kernel, False, cap), grid=(steps,),...  15.1 us
    pallas_call x1, Pallas kernels, body(): pl.pallas_call(functools.partial(pull_kernel, True), grid=(steps,), out_s...  14.4 us
    pallas_call x1, Pallas kernels, body(): pl.pallas_call(functools.partial(pull_kernel, False), grid=(steps,), out_...  13.2 us
    pallas_call x1, Pallas kernels, body(): pl.pallas_call(functools.partial(count_seeds, columns), out_shape=shape(v...  8.41 us
  transfers between devices with their start and end apart: 1, of which 0 were waited for; matrix products, arithmetic and copies ran while one was open for 0% of the time, Pallas kernels for 7%

profile of v5, /device:TPU:1, one launch (start us, length us, event | category | flops | bytes accessed | tf_op | source)
XLA Modules:
  0.0 335.9 jit_solution(16239207312194530448)
XLA Ops:
  0.6 1.3 all_to_all.7
  2.0 5.2 %all-to-all-start = ((s32[8,1,16]{2,1,0:T(1,128)}), s32[8,1,16]{2,1,0:T(1,128)S(1)}, u32[]{:S(2)}, u32[]{:S(2)}) async-start(s32[8,1,16]{2,1,0:T(1,128)} %bitcast), calls=%async_computation | async-start | bytes 8192 | tf_op jit(solution)/shard_map/all_to_all | solution.py:429
  7.2 1.5 copy.11.refs_0_
  8.7 8.4 %shard_map.86.refs_2_.refs_3_.good_ref = f32[16,128,128]{2,1,0:T(8,128)} custom-call(s32[128,128]{1,0:T(8,128)} %source.1), custom_call_target="tpu_custom_call" | custom-call | tf_op jit(solution)/shard_map/pallas_call | solution.py:432
  17.1 16.5 %shard_map.87.words_ref = s16[32,528,128]{2,1,0:T(8,128)(2,1)} custom-call(s32[256]{0:T(256)} %refs_0_.8, s32[256]{0:T(256)} %refs_1_.7, f32[16,128,128]{2,1,0:T(8,128)} %shard_map.86.refs_2_.refs_3_.good_ref, s32[16,1,128]{2,1,0:T(1,128)} %bitcast.7, bf16[256,128,128]{2,1,0:T(8,128)(2,1)} %refs_4_.3), custom_call_target="tpu_custom_call" | custom-call | tf_op jit(solution)/shard_map/pallas_call | solution.py:441
  33.5 0.0 all-to-all-done
  33.5 0.0 copy-start
  33.6 0.6 copy-done
  34.1 72.8 %shard_map.88 = (f32[16,128,128]{2,1,0:T(8,128)}, f32[16,1,128]{2,1,0:T(1,128)}, f32[16,128,128]{2,1,0:T(8,128)}) custom-call(s32[8,16]{1,0:T(8,128)} %bitcast.3, s16[32,528,128]{2,1,0:T(8,128)(2,1)} %shard_map.87.words_ref, s32[128,64]{1,0:T(8,128)} %copy.11.refs_0_), custom_call_target="tpu_custom_call" | custom-call | tf_op jit(solution)/shard_map/pallas_call | solution.py:455
  107.0 15.1 %shard_map.89.words_ref = s16[32,528,128]{2,1,0:T(8,128)(2,1)} custom-call(s32[256]{0:T(256)} %refs_0_.8, s32[256]{0:T(256)} %refs_1_.7, f32[16,128,128]{2,1,0:T(8,128)} %get-tuple-element.8.refs_2_, f32[16,128,128]{2,1,0:T(8,128)} %shard_map.86.refs_2_.refs_3_.good_ref, s32[16,1,128]{2,1,0:T(1,128)} %bitcast.8, bf16[256,128,128]{2,1,0:T(8,128)(2,1)} %refs_4_.3), custom_call_target="tpu_custom_call" | custom-call | tf_op jit(solution)/shard_map/pallas_call | solution.py:480
  122.1 70.0 %shard_map.90.inflow = f32[16,128,128]{2,1,0:T(8,128)} custom-call(s32[8,16]{1,0:T(8,128)} %bitcast.4, s16[32,528,128]{2,1,0:T(8,128)(2,1)} %shard_map.89.words_ref), custom_call_target="tpu_custom_call" | custom-call | tf_op jit(solution)/shard_map/pallas_call | solution.py:455
  192.1 5.3 %shard_map.91 = (f32[2048,128]{1,0:T(8,128)}, f32[16,128,128]{2,1,0:T(8,128)}, bf16[16,128,128]{2,1,0:T(8,128)(2,1)}) custom-call(f32[16,128,128]{2,1,0:T(8,128)} %shard_map.90.inflow, f32[16,128,128]{2,1,0:T(8,128)} %shard_map.86.refs_2_.refs_3_.good_ref, f32[16,128,128]{2,1,0:T(8,128)} %get-tuple-element.9.spam_ref.refs_3_, ...), custom_call_target="tpu_custom_call" | custom-call | tf_op jit(solution)/shard_map/pallas_call | solution.py:507
  197.4 54.8 %shard_map.92.refs_2_ = bf16[128,128,128]{2,1,0:T(8,128)(2,1)} custom-call(s32[8,16]{1,0:T(8,128)} %bitcast.5, bf16[16,128,128]{2,1,0:T(8,128)(2,1)} %get-tuple-element.12.share_ref), custom_call_target="tpu_custom_call" | custom-call | tf_op jit(solution)/shard_map/pallas_call | solution.py:513
  252.2 13.2 %shard_map.93.share_ref = bf16[16,128,128]{2,1,0:T(8,128)(2,1)} custom-call(s32[256]{0:T(256)} %refs_0_.8, s32[256]{0:T(256)} %refs_1_.7, bf16[128,128,128]{2,1,0:T(8,128)(2,1)} %shard_map.92.refs_2_, f32[16,128,128]{2,1,0:T(8,128)} %get-tuple-element.9.spam_ref.refs_3_, f32[16,128,128]{2,1,0:T(8,128)} %get-tuple-element.13.refs_4_, ...), custom_call_target="tpu_custom_call" | custom-call | tf_op jit(solution)/shard_map/pallas_call | solution.py:514
  265.4 56.1 %shard_map.94.refs_2_ = bf16[128,128,128]{2,1,0:T(8,128)(2,1)} custom-call(s32[8,16]{1,0:T(8,128)} %bitcast.6, bf16[16,128,128]{2,1,0:T(8,128)(2,1)} %shard_map.93.share_ref), custom_call_target="tpu_custom_call" | custom-call | tf_op jit(solution)/shard_map/pallas_call | solution.py:522
  321.5 14.4 %shard_map.95 = f32[2048,128]{1,0:T(8,128)} custom-call(s32[256]{0:T(256)} %refs_0_.8, s32[256]{0:T(256)} %refs_1_.7, bf16[128,128,128]{2,1,0:T(8,128)(2,1)} %shard_map.94.refs_2_, f32[16,128,128]{2,1,0:T(8,128)} %get-tuple-element.9.spam_ref.refs_3_, bf16[256,128,128]{2,1,0:T(8,128)(2,1)} %refs_4_.3), custom_call_target="tpu_custom_call" | custom-call | tf_op jit(solution)/shard_map/pallas_call | solution.py:523
Async XLA Ops:
  2.0 31.6 %all-to-all-start = ((s32[8,1,16]{2,1,0:T(1,128)}), s32[8,1,16]{2,1,0:T(1,128)S(1)}, u32[]{:S(2)}, u32[]{:S(2)}) async-start(s32[8,1,16]{2,1,0:T(1,128)} %bitcast), calls=%async_computation | async-start | bytes 8192 | tf_op jit(solution)/shard_map/all_to_all | solution.py:429
  33.5 0.6 copy-start
